TPU v7x, 32 devices: a whole 2x2x4 slice. The times are simulated.
32 devices in a mesh: dp: 8 (over y, x, core), tensor: 4 (over z).
Axes of the slice: x: 2, y: 2, z: 4, core: 2. Of those that a mesh axis runs over, the one named last changes fastest.
Arguments:
- layer_inputs: bfloat16 [256, 8192], P(None, ('dp', 'tensor')), may hold values from -6 to 6
- policy_query_weight: bfloat16 [8192, 8192], P('dp', 'tensor'), may hold values from -0.0625 to 0.0625
- policy_key_value: bfloat16 [8192, 8, 256], P('dp', 'tensor'), may hold values from -0.0625 to 0.0625
- policy_out: bfloat16 [8192, 8192], P('tensor', 'dp'), may hold values from -0.0625 to 0.0625
- kv_cache: bfloat16 [256, 256, 8, 256], P('dp', None, 'tensor'), may hold values from -400 to 400
- prefix_len: int32 [256], P('dp'), may hold values from 1 to 256, 32768 in all
- responses: bfloat16 [128, 16, 8192], P('dp'), may hold values from -11 to 11
- response_len: int32 [128], P('dp'), may hold values from 1 to 16, 1024 in all
- assign: int32 [128, 1], P('dp'), may hold values from 0 to 7; in each aligned block of 16 rows (0 to 15, 16 to 31, ...) at most 2 rows name the same one
- critic_query_weight: bfloat16 [8192, 8192], P('dp', 'tensor'), may hold values from -1 to 1
- critic_key_value: bfloat16 [8192, 8, 256], P('dp', 'tensor'), may hold values from -1 to 1
- score_weight: bfloat16 [8192], P('tensor'), may hold values from -0.0625 to 0.0625
Outputs:
- decode_out: bfloat16 [2, 256, 8192], P(None, None, ('dp', 'tensor'))
- values: float32 [8, 16, 16], P('dp')
Inputs may be any that keep to these rules, and one draw needn't show every extreme that they name: `assign`: within the rows of one dp device at most 2 rows name the same shard, and this bound is reached.
All inputs are finite; a program needn't handle non-finite values. No bound on the sum of `prefix_len` or of `response_len` on one device may be relied on, other than what follows from the above.
Results may differ from a plain program's by a relative error of at most 0.0078.
Values may be sent and summed in bfloat16 or wider, within the bound.
No kernel may reach another device: no remote copies, remote signals or barrier semaphores. Data moves between devices by JAX's collectives and lax.ppermute only.
A program may use at most 192 MiB of HBM per device.

v0:
```python
import jax
import jax.numpy as jnp
from jax import lax
from jax.sharding import PartitionSpec as P

QUERY_HEADS = 64
KEY_HEADS = 8
HEAD_DIM = 128
STEPS = 2
CAPR = 2


def step_term(gathered, joined):
    return lax.psum_scatter(
        jnp.dot(gathered, joined, preferred_element_type=jnp.float32),
        "dp",
        scatter_dimension=0,
        tiled=True,
    )


def critic_values(slot_queries, slot_pairs, lengths, score_weight):
    rows_count = slot_queries.shape[0]
    tok_len = slot_queries.shape[1]
    scale_factor = HEAD_DIM ** (-0.5)
    scores = (
        jnp.einsum(
            "stkgd,sukd->skgtu",
            slot_queries,
            slot_pairs[..., :HEAD_DIM],
            preferred_element_type=jnp.float32,
        )
        * scale_factor
    )
    later = lax.broadcasted_iota(jnp.int32, (tok_len, tok_len), 1)
    earlier = lax.broadcasted_iota(jnp.int32, (tok_len, tok_len), 0)
    allowed = (later[None] <= earlier[None]) & (later[None] < lengths[:, None, None])
    scores = jnp.where(allowed[:, None, None], scores, -1e30)
    top = jnp.max(scores, -1, keepdims=True)
    expo = jnp.exp(scores - top)
    weights = (expo / jnp.sum(expo, -1, keepdims=True)).astype(jnp.bfloat16)
    mixed = jnp.einsum(
        "skgtu,sukd->stkgd", weights, slot_pairs[..., HEAD_DIM:], preferred_element_type=jnp.float32
    )
    mixed = mixed.astype(jnp.bfloat16).reshape(rows_count, tok_len, -1)
    partial_values = jnp.dot(mixed, score_weight, preferred_element_type=jnp.float32)
    token_values = lax.psum(partial_values, "tensor")
    valid = lax.broadcasted_iota(jnp.int32, (rows_count, tok_len), 1) < lengths[:, None]
    return jnp.where(valid, token_values, 0.0)


def per_device(
    layer_inputs,
    policy_query_weight,
    policy_key_value,
    policy_out,
    kv_cache,
    prefix_len,
    responses,
    response_len,
    assign,
    critic_query_weight,
    critic_key_value,
    score_weight,
):
    shards = lax.axis_size("dp")
    rows_here = kv_cache.shape[0]
    kv_here = kv_cache.shape[2]
    group_index = QUERY_HEADS // KEY_HEADS
    scale_factor = HEAD_DIM ** (-0.5)
    width_here = policy_query_weight.shape[0]
    q_width = policy_query_weight.shape[1]
    joined = jnp.concatenate(
        [policy_query_weight, policy_key_value.reshape(width_here, -1)], axis=1
    )
    cache_keys = kv_cache[..., :HEAD_DIM]
    cache_values = kv_cache[..., HEAD_DIM:]
    cache_mask = (
        lax.broadcasted_iota(jnp.int32, (rows_here, kv_cache.shape[1]), 1) < prefix_len[:, None]
    )
    current_state = layer_inputs
    fresh_entries = []
    outputs = []
    for step in range(STEPS):
        gathered = lax.all_gather(current_state, "tensor", axis=1, tiled=True)
        projected = step_term(gathered, joined).astype(jnp.bfloat16)
        query_rows = projected[:, :q_width].reshape(rows_here, kv_here, group_index, HEAD_DIM)
        fresh_entries.append(projected[:, q_width:].reshape(rows_here, kv_here, 2 * HEAD_DIM))
        fresh_all = jnp.stack(fresh_entries)
        new_keys = fresh_all[:, :, :, :HEAD_DIM]
        new_values = fresh_all[:, :, :, HEAD_DIM:]
        old_scores = (
            jnp.einsum(
                "rkgd,rckd->rkgc", query_rows, cache_keys, preferred_element_type=jnp.float32
            )
            * scale_factor
        )
        old_scores = jnp.where(cache_mask[:, None, None, :], old_scores, -1e30)
        new_scores = (
            jnp.einsum("rkgd,trkd->rkgt", query_rows, new_keys, preferred_element_type=jnp.float32)
            * scale_factor
        )
        top = jnp.maximum(jnp.max(old_scores, -1), jnp.max(new_scores, -1))
        old_exp = jnp.exp(old_scores - top[..., None])
        new_exp = jnp.exp(new_scores - top[..., None])
        total = jnp.sum(old_exp, -1) + jnp.sum(new_exp, -1)
        old_weights = (old_exp / total[..., None]).astype(jnp.bfloat16)
        new_weights = (new_exp / total[..., None]).astype(jnp.bfloat16)
        mixed = jnp.einsum(
            "rkgc,rckd->rkgd", old_weights, cache_values, preferred_element_type=jnp.float32
        )
        mixed = mixed + jnp.einsum(
            "rkgt,trkd->rkgd", new_weights, new_values, preferred_element_type=jnp.float32
        )
        attended = mixed.astype(jnp.bfloat16).reshape(rows_here, -1)
        term = jnp.dot(
            lax.all_gather(attended, "dp", axis=0, tiled=True),
            policy_out,
            preferred_element_type=jnp.float32,
        )
        summed = lax.psum_scatter(term, "tensor", scatter_dimension=1, tiled=True)
        current_state = (current_state.astype(jnp.float32) + summed).astype(jnp.bfloat16)
        outputs.append(current_state)
    decode_out = jnp.stack(outputs)
    rows_source = responses.shape[0]
    tok_len = responses.shape[1]
    model_width = responses.shape[2]
    dest = assign[:, 0]
    onehot = (dest[:, None] == lax.broadcasted_iota(jnp.int32, (1, shards), 1)).astype(jnp.int32)
    rank = jnp.sum((jnp.cumsum(onehot, 0) - onehot) * onehot, 1)
    slot_index = dest * CAPR + rank
    select_int = (
        lax.broadcasted_iota(jnp.int32, (shards * CAPR, rows_source), 0) == slot_index[None, :]
    ).astype(jnp.int32)
    select = select_int.astype(jnp.bfloat16)
    packed_len = jnp.sum(select_int * response_len[None, :], 1).reshape(shards, CAPR)
    kv_width = critic_key_value.shape[1] * critic_key_value.shape[2]

    def make_fold(token_rows):

        def add_rows(totals, pieces, start):
            first = jnp.dot(token_rows, pieces[0], preferred_element_type=jnp.float32)
            second = jnp.dot(
                token_rows,
                pieces[1].reshape(pieces[1].shape[0], -1),
                preferred_element_type=jnp.float32,
            )
            return (first, second)

        start_values = (
            jnp.zeros((token_rows.shape[0], q_width), jnp.float32),
            jnp.zeros((token_rows.shape[0], kv_width), jnp.float32),
        )
        return (add_rows, start_values)

    packed = jnp.dot(select, responses.reshape(rows_source, -1), preferred_element_type=jnp.float32)
    packed = packed.astype(jnp.bfloat16).reshape(shards, CAPR, tok_len, model_width)
    arrived, lengths = (
        lax.all_to_all(packed, "dp", split_axis=0, concat_axis=0, tiled=True),
        lax.all_to_all(packed_len, "dp", split_axis=0, concat_axis=0, tiled=True),
    )
    token_rows = arrived.reshape(-1, model_width)
    add_rows, start_values = make_fold(token_rows)
    slot_q, slot_kv = add_rows(
        start_values,
        (
            lax.all_gather(critic_query_weight, "dp", axis=0, tiled=True),
            lax.all_gather(critic_key_value, "dp", axis=0, tiled=True),
        ),
        jnp.int32(0),
    )
    slot_queries = slot_q.astype(jnp.bfloat16).reshape(
        shards * CAPR, tok_len, kv_here, group_index, HEAD_DIM
    )
    slot_pairs = slot_kv.astype(jnp.bfloat16).reshape(shards * CAPR, tok_len, kv_here, 2 * HEAD_DIM)
    token_values = critic_values(slot_queries, slot_pairs, lengths.reshape(-1), score_weight)
    values_out = token_values.reshape(1, shards * CAPR, tok_len)
    return (decode_out, values_out)


def solution(mesh):
    return jax.shard_map(
        per_device,
        mesh=mesh,
        in_specs=(
            P(None, ("dp", "tensor")),
            P("dp", "tensor"),
            P("dp", "tensor", None),
            P("tensor", "dp"),
            P("dp", None, "tensor", None),
            P("dp"),
            P("dp", None, None),
            P("dp"),
            P("dp", None),
            P("dp", "tensor"),
            P("dp", "tensor", None),
            P("tensor"),
        ),
        out_specs=(P(None, None, ("dp", "tensor")), P("dp", None, None)),
        check_vma=False,
    )
```

profile of v0, /device:TPU:0, one launch (start us, length us, event | category | flops | bytes accessed | tf_op | source)
XLA Modules:
  0.0 573.1 jit_solution(13776555866520422679)
XLA Ops:
  10.1 17.4 %all_gather.18 = bf16[256,1024]{1,0:T(8,128)(2,1)S(1)} all-gather(bf16[256,256]{1,0:T(8,128)(2,1)S(1)} %copy-done.3), channel_id=1, replica_groups=mesh['dp'=8,'tensor'=4] {'tensor'}, dimensions={1}, use_global_device_ids=true | all-gather | bytes 655360 | tf_op jit(solution)/shard_map/all_gather | solution.py:85
  33.7 8.5 %fusion.73 = (bf16[32,256,2,128]{3,2,1,0:T(2,128)(2,1)}, bf16[32,256,2,128]{3,2,1,0:T(2,128)(2,1)}) fusion(bf16[32,256,2,256]{3,2,1,0:T(2,128)(2,1)} %param.16), kind=kLoop, calls=%fused_computation.93 | loop fusion | bytes 16777216 | tf_op jit(solution)/shard_map/slice | solution.py:76
  42.2 36.8 %reduce-scatter.13.cloned.1.call-done = f32[32,2560]{1,0:T(8,128)} async-done(((f32[256,2560]{1,0:T(8,128)}), f32[32,2560]{1,0:T(8,128)}) %reduce-scatter.13.cloned.1.call-update) | async-done | bytes 327696
  81.9 3.5 fusion.76
  89.9 23.5 %all-gather.5.cloned.1.call-done = bf16[256,2048]{1,0:T(8,128)(2,1)} async-done(((bf16[32,2048]{1,0:T(8,128)(2,1)}), bf16[256,2048]{1,0:T(8,128)(2,1)}) %all-gather.5.cloned.1.call-update) | async-done | bytes 1048592 | tf_op jit(solution)/shard_map/all_gather | solution.py:117
  113.4 4.7 fusion.82
  118.2 27.4 %reduce-scatter.7.cloned.1.call-done = f32[256,256]{1,0:T(8,128)} async-done(((f32[256,1024]{1,0:T(8,128)}), f32[256,256]{1,0:T(8,128)}) %reduce-scatter.7.cloned.1.call-update) | async-done | bytes 262160 | tf_op jit(solution)/shard_map/reduce_scatter | solution.py:121
  146.6 16.0 %all_gather.20 = bf16[256,1024]{1,0:T(8,128)(2,1)S(1)} all-gather(bf16[256,256]{1,0:T(8,128)(2,1)S(1)} %add_convert_fusion.1), channel_id=1, replica_groups=mesh['dp'=8,'tensor'=4] {'tensor'}, dimensions={1}, use_global_device_ids=true | all-gather | bytes 655360 | tf_op jit(solution)/shard_map/all_gather | solution.py:85
  162.6 5.5 fusion.83
  168.3 41.8 %reduce-scatter.9.cloned.1.call-done = f32[32,2560]{1,0:T(8,128)} async-done(((f32[256,2560]{1,0:T(8,128)}), f32[32,2560]{1,0:T(8,128)}) %reduce-scatter.9.cloned.1.call-update) | async-done | bytes 327696 | tf_op jit(solution)/shard_map/reduce_scatter | solution.py:14
  211.2 3.6 fusion.77
  218.1 22.7 %all-gather.7.cloned.1.call-done = bf16[256,2048]{1,0:T(8,128)(2,1)} async-done(((bf16[32,2048]{1,0:T(8,128)(2,1)}), bf16[256,2048]{1,0:T(8,128)(2,1)}) %all-gather.7.cloned.1.call-update) | async-done | bytes 1048592 | tf_op jit(solution)/shard_map/all_gather | solution.py:117
  240.8 4.7 fusion.84
  250.8 4.8 copy.128
  256.8 4.2 copy.129
  261.1 4.9 all-to-all-start.1
  267.4 59.8 %all-gather.9.cloned.1.call-done = bf16[8192,2,256]{2,1,0:T(2,128)(2,1)} async-done(((bf16[1024,2,256]{2,1,0:T(2,128)(2,1)}), bf16[8192,2,256]{2,1,0:T(2,128)(2,1)}) %all-gather.9.cloned.1.call-update) | async-done | bytes 8388624 | tf_op jit(solution)/shard_map/all_gather | solution.py:168
  327.2 8.0 %copy.130 = bf16[1024,8,2,256]{3,1,2,0:T(8,128)(2,1)} copy(bf16[1024,8,2,256]{3,2,1,0:T(2,128)(2,1)} %bitcast.115) | data formatting | bytes 16777216
  337.5 7.0 %convolution_convert_fusion.3 = bf16[256,512]{1,0:T(8,128)(2,1)S(1)} fusion(bf16[256,8192]{1,0:T(8,128)(2,1)} %bitcast.11, bf16[8192,512]{1,0:T(8,128)(2,1)} %bitcast.116), kind=kOutput, calls=%fused_computation.23 | convolution fusion | flops 2147614720 | bytes 12845056 | tf_op jit(solution)/shard_map/dot_general | solution.py:143
  344.7 23.3 %reduce-scatter.11.cloned.1.call-done = f32[256,256]{1,0:T(8,128)} async-done(((f32[256,1024]{1,0:T(8,128)}), f32[256,256]{1,0:T(8,128)}) %reduce-scatter.11.cloned.1.call-update) | async-done | bytes 262160 | tf_op jit(solution)/shard_map/reduce_scatter | solution.py:121
  369.7 159.4 %all-gather.11.cloned.1.call-done = bf16[8192,2048]{1,0:T(8,128)(2,1)} async-done(((bf16[1024,2048]{1,0:T(8,128)(2,1)}), bf16[8192,2048]{1,0:T(8,128)(2,1)}) %all-gather.11.cloned.1.call-update) | async-done | bytes 33554448 | tf_op jit(solution)/shard_map/all_gather | solution.py:167
  529.1 16.2 %fusion.11 = bf16[32,8,16,128]{3,1,2,0:T(8,128)(2,1)S(1)} fusion(bf16[256,8192]{1,0:T(8,128)(2,1)} %bitcast.11, bf16[8192,2048]{1,0:T(8,128)(2,1)} %all-gather.11.cloned.1.call-done), kind=kOutput, calls=%fused_computation.18 | convolution fusion | flops 8590458880 | bytes 38797312 | tf_op jit(solution)/shard_map/dot_general | solution.py:142
  545.6 4.0 fusion.79
  553.7 11.8 %psum.7 = f32[16,16]{1,0:T(8,128)S(1)} all-reduce(f32[16,16]{1,0:T(8,128)S(1)} %bitcast.131), channel_id=1, replica_groups=mesh['dp'=8,'tensor'=4] {'tensor'}, use_global_device_ids=true, to_apply=%region_15.16 | all-reduce | flops 256 | bytes 2048 | tf_op jit(solution)/shard_map/psum | solution.py:47
  (100 shorter events, 39.0 us)
Async XLA Ops:
  7.2 2.7 copy-start.2
  7.2 2.9 copy-start.3
  7.2 71.9 %reduce-scatter.13.cloned.1.call-start = ((), (), s32[]{:S(2)}) async-start(), calls=%async_computation.13 | async-start | bytes 2949120
  27.6 2.3 copy-start.1
  31.5 2.2 copy-start.6
  33.6 79.8 %all-gather.5.cloned.1.call-start = ((), (), s32[]{:S(2)}) async-start(), calls=%async_computation.6 | async-start | bytes 1179648 | tf_op jit(solution)/shard_map/all_gather | solution.py:117
  89.9 55.7 %reduce-scatter.7.cloned.1.call-start = ((), (), s32[]{:S(2)}) async-start(), calls=%async_computation.7 | async-start | bytes 1310720 | tf_op jit(solution)/shard_map/reduce_scatter | solution.py:121
  118.2 91.9 %reduce-scatter.9.cloned.1.call-start = ((), (), s32[]{:S(2)}) async-start(), calls=%async_computation.8 | async-start | bytes 2949120 | tf_op jit(solution)/shard_map/reduce_scatter | solution.py:14
  168.1 72.7 %all-gather.7.cloned.1.call-start = ((), (), s32[]{:S(2)}) async-start(), calls=%async_computation.9 | async-start | bytes 1179648 | tf_op jit(solution)/shard_map/all_gather | solution.py:117
  211.2 4.7 copy-start
  217.3 109.9 %all-gather.9.cloned.1.call-start = ((), (), s32[]{:S(2)}) async-start(), calls=%async_computation.11 | async-start | bytes 9437184 | tf_op jit(solution)/shard_map/all_gather | solution.py:168
  217.9 150.1 %reduce-scatter.11.cloned.1.call-start = ((), (), s32[]{:S(2)}) async-start(), calls=%async_computation.10 | async-start | bytes 1310720 | tf_op jit(solution)/shard_map/reduce_scatter | solution.py:121
  245.6 0.8 copy-start.5
  245.6 1.1 copy-start.7
  245.6 283.5 %all-gather.11.cloned.1.call-start = ((), (), s32[]{:S(2)}) async-start(), calls=%async_computation.12 | async-start | bytes 37748736 | tf_op jit(solution)/shard_map/all_gather | solution.py:167
  247.5 13.6 %all-to-all-start = ((s32[8,1,2]{2,1,0:T(1,128)}), s32[8,1,2]{2,1,0:T(1,128)S(1)}, u32[]{:S(2)}, u32[]{:S(2)}) async-start(s32[8,1,2]{2,1,0:T(1,128)} %bitcast.10), calls=%async_computation.3 | async-start | bytes 8192 | tf_op jit(solution)/shard_map/all_to_all | solution.py:160
  261.1 4.9 copy-start.4
  261.1 76.4 %all-to-all-start.1 = ((bf16[8,2,16,8192]{3,2,1,0:T(8,128)(2,1)}), bf16[8,2,16,8192]{3,2,1,0:T(8,128)(2,1)}, u32[]{:S(2)}, u32[]{:S(2)}) async-start(bf16[8,2,16,8192]{3,2,1,0:T(8,128)(2,1)} %bitcast.114), calls=%async_computation.4 | async-start | bytes 8388608 | tf_op jit(solution)/shard_map/all_to_all | solution.py:159
Sparse Core Ops, SparseCore 0:
  33.7 45.2 reduce-scatter.12
  90.0 23.3 all-gather.4
  118.3 27.2 reduce-scatter.6
  168.2 41.8 reduce-scatter.8
  217.4 23.3 all-gather.6
  242.6 84.5 all-gather.8
  329.5 38.5 reduce-scatter.10
  369.9 159.1 all-gather.10
where the time goes:
time: 574 us; the launch traced here: 573 us
  waiting for transfers between devices  398 us (69%)
  matrix products  59.9 us (10%)
  blocking collectives  45.2 us (8%)
  local copies, waits for them, and re-layouts  40.1 us (7%)
  between operations  14.5 us (3%)
  starting transfers between devices  8.73 us (2%)
  other arithmetic  6.37 us (1%)
    all_gather x1, waiting for transfers between devices, per_device(): lax.all_gather(critic_query_weight, 'dp', axis=0, tiled=True)  159 us
    all_gather x1, waiting for transfers between devices, per_device(): lax.all_gather(critic_key_value, 'dp', axis=0, tiled=True)  59.8 us
    reduce_scatter x2, waiting for transfers between devices, per_device(): summed = lax.psum_scatter(term, 'tensor', scatter_dimension=1, tiled=True)  50.7 us
    all_gather x2, waiting for transfers between devices, per_device(): lax.all_gather(attended, 'dp', axis=0, tiled=True)  46.2 us
    reduce_scatter x1, waiting for transfers between devices, step_term(): lax.psum_scatter(jnp.dot(gathered, joined, preferred_element_type=jnp.flo...  41.8 us
    unnamed x9, waiting for transfers between devices  38.2 us
    all_gather x2, blocking collectives, per_device(): gathered = lax.all_gather(current_state, 'tensor', axis=1, tiled=True)  33.4 us
    unnamed x31, local copies, waits for them, and re-layouts  26.5 us
  transfers between devices with their start and end apart: 10, of which 9 were waited for; matrix products, arithmetic and copies ran while one was open for 7% of the time, Pallas kernels for 0%

commit v1 on v0

v1 whole, which is shorter than its diff:
```python
import jax
import jax.numpy as jnp
from jax import lax
from jax.sharding import Mesh, PartitionSpec as P

QUERY_HEADS = 64
KEY_HEADS = 8
HEAD_DIM = 128
STEPS = 2
CAPR = 2
F32 = jnp.float32
BF16 = jnp.bfloat16
SCALE = HEAD_DIM ** (-0.5)


def dot(a, b):
    return jnp.dot(a, b, preferred_element_type=F32)


def swap(x):
    return lax.ppermute(x, "core", [(0, 1), (1, 0)])


def exchange(pieces, axes):
    return lax.all_to_all(pieces, axes, 0, 0, tiled=True)


def add_up(pieces):
    total = pieces[0].astype(F32)
    for i in range(1, pieces.shape[0]):
        total = total + pieces[i].astype(F32)
    return total


def pick(x, index, axis):
    return lax.dynamic_index_in_dim(x, index, axis, keepdims=False)


def cached_attention(q, cache_keys, cache_values, cache_mask, new_keys, new_values):
    old_scores = jnp.einsum("rkgd,rckd->rkgc", q, cache_keys, preferred_element_type=F32) * SCALE
    old_scores = jnp.where(cache_mask[:, None, None, :], old_scores, -1e30)
    new_scores = jnp.einsum("rkgd,trkd->rkgt", q, new_keys, preferred_element_type=F32) * SCALE
    top = jnp.maximum(jnp.max(old_scores, -1), jnp.max(new_scores, -1))
    old_exp = jnp.exp(old_scores - top[..., None])
    new_exp = jnp.exp(new_scores - top[..., None])
    total = jnp.sum(old_exp, -1) + jnp.sum(new_exp, -1)
    old_weights = (old_exp / total[..., None]).astype(BF16)
    new_weights = (new_exp / total[..., None]).astype(BF16)
    mixed = jnp.einsum("rkgc,rckd->rkgd", old_weights, cache_values, preferred_element_type=F32)
    mixed = mixed + jnp.einsum("rkgt,trkd->rkgd", new_weights, new_values, preferred_element_type=F32)
    return mixed.astype(BF16)


def critic_partials(queries, pairs, lengths, score_weight):
    rows, tok_len = queries.shape[:2]
    scores = (
        jnp.einsum("stkgd,sukd->skgtu", queries, pairs[..., :HEAD_DIM], preferred_element_type=F32)
        * SCALE
    )
    later = lax.broadcasted_iota(jnp.int32, (tok_len, tok_len), 1)
    earlier = lax.broadcasted_iota(jnp.int32, (tok_len, tok_len), 0)
    allowed = (later[None] <= earlier[None]) & (later[None] < lengths[:, None, None])
    scores = jnp.where(allowed[:, None, None], scores, -1e30)
    top = jnp.max(scores, -1, keepdims=True)
    expo = jnp.exp(scores - top)
    weights = (expo / jnp.sum(expo, -1, keepdims=True)).astype(BF16)
    mixed = jnp.einsum("skgtu,sukd->stkgd", weights, pairs[..., HEAD_DIM:], preferred_element_type=F32)
    mixed = mixed.astype(BF16).reshape(rows, tok_len, -1)
    partial_values = dot(mixed, score_weight)
    valid = lax.broadcasted_iota(jnp.int32, (rows, tok_len), 1) < lengths[:, None]
    return jnp.where(valid, partial_values, 0.0)


def per_device(
    layer_inputs,
    policy_query_weight,
    policy_key_value,
    policy_out,
    kv_cache,
    prefix_len,
    responses,
    response_len,
    assign,
    critic_query_weight,
    critic_key_value,
    score_weight,
):
    chips = lax.axis_size("chip")
    zs = lax.axis_size("tensor")
    core = lax.axis_index("core")
    shards = chips * 2
    rows = kv_cache.shape[0]
    heads = kv_cache.shape[2]
    group = QUERY_HEADS // KEY_HEADS
    width = policy_query_weight.shape[0]
    q_width = policy_query_weight.shape[1]
    piece = layer_inputs.shape[1]
    half = chips * rows

    src_rows, tok_len, model_width = responses.shape
    tokens = src_rows * tok_len
    split = responses.reshape(tokens, chips, 2, width)
    tok_mine = exchange(pick(split, core, 2).transpose(1, 0, 2), "chip")
    tok_other = exchange(pick(split, 1 - core, 2).transpose(1, 0, 2), "chip")

    pk = policy_key_value.reshape(width, -1)
    wq, wk, wo = (policy_query_weight, swap(policy_query_weight)), (pk, swap(pk)), (policy_out, swap(policy_out))
    cache_keys = kv_cache[..., :HEAD_DIM]
    cache_values = kv_cache[..., HEAD_DIM:]
    cache_mask = lax.broadcasted_iota(jnp.int32, (rows, kv_cache.shape[1]), 1) < prefix_len[:, None]

    by_core = layer_inputs.reshape(chips, 2, rows, piece)
    kept = pick(by_core, core, 1).reshape(half, piece)
    got = swap(pick(by_core, 1 - core, 1).reshape(half, piece))
    state = jnp.concatenate([kept, got], 1)
    fresh = []
    outputs = []
    for step in range(STEPS):
        spread = exchange(jnp.broadcast_to(state[None], (zs, half, 2 * piece)), "tensor")
        spread = spread.reshape(zs, half, 2, piece).transpose(2, 1, 0, 3).reshape(2, half, width)
        q_part = (dot(spread[0], wq[0]) + dot(spread[1], wq[1])).astype(BF16)
        k_part = (dot(spread[0], wk[0]) + dot(spread[1], wk[1])).astype(BF16)
        part = jnp.concatenate([q_part, k_part], 1)
        projected = add_up(exchange(part.reshape(chips, rows, -1), "chip")).astype(BF16)
        q = projected[:, :q_width].reshape(rows, heads, group, HEAD_DIM)
        fresh.append(projected[:, q_width:].reshape(rows, heads, 2 * HEAD_DIM))
        fresh_all = jnp.stack(fresh)
        attended = cached_attention(
            q, cache_keys, cache_values, cache_mask, fresh_all[..., :HEAD_DIM], fresh_all[..., HEAD_DIM:]
        ).reshape(rows, q_width)
        gathered = exchange(jnp.broadcast_to(attended[None], (chips, rows, q_width)), "chip").reshape(half, q_width)
        mine = dot(gathered, wo[0]).astype(BF16).reshape(half, zs, piece)
        other = dot(gathered, wo[1]).astype(BF16).reshape(half, zs, piece)
        term = jnp.concatenate([mine, other], 2).transpose(1, 0, 2)
        summed = add_up(exchange(term, "tensor"))
        state = (state.astype(F32) + summed).astype(BF16)
        back = swap(state[:, piece:]).reshape(chips, 1, rows, piece)
        own = state[:, :piece].reshape(chips, 1, rows, piece)
        both = jnp.where(core == 0, jnp.concatenate([own, back], 1), jnp.concatenate([back, own], 1))
        outputs.append(both.reshape(shards * rows, piece))
    decode_out = jnp.stack(outputs)

    ck = critic_key_value.reshape(width, -1)
    ck_other = swap(ck)
    cq_other = swap(critic_query_weight)
    tm = tok_mine.reshape(chips * tokens, width)
    to = tok_other.reshape(chips * tokens, width)
    kv_part = (dot(tm, ck) + dot(to, ck_other)).astype(BF16)
    q_part = (dot(tm, critic_query_weight) + dot(to, cq_other)).astype(BF16)
    slot_kv = add_up(exchange(kv_part.reshape(chips, tokens, -1), "chip")).astype(BF16)
    slot_q = add_up(exchange(q_part.reshape(chips, tokens, -1), "chip")).astype(BF16)
    partial_values = critic_partials(
        slot_q.reshape(src_rows, tok_len, heads, group, HEAD_DIM),
        slot_kv.reshape(src_rows, tok_len, heads, 2 * HEAD_DIM),
        response_len,
        score_weight,
    )
    dest = assign[:, 0]
    onehot = (dest[:, None] == lax.broadcasted_iota(jnp.int32, (1, shards), 1)).astype(jnp.int32)
    rank = jnp.sum((jnp.cumsum(onehot, 0) - onehot) * onehot, 1)
    slot = dest * CAPR + rank
    chosen = lax.broadcasted_iota(jnp.int32, (shards * CAPR, src_rows), 0) == slot[None, :]
    packed = jnp.sum(jnp.where(chosen[:, :, None], partial_values[None], 0.0), 1)
    packed = jnp.broadcast_to(packed.reshape(shards, 1, CAPR, tok_len), (shards, zs, CAPR, tok_len))
    arrived = exchange(packed.reshape(shards * zs, CAPR, tok_len), ("chip", "core", "tensor"))
    values = jnp.sum(arrived.reshape(shards, zs, CAPR, tok_len), 1)
    return decode_out, values.reshape(1, shards * CAPR, tok_len)


def solution(mesh):
    dp, tensor = mesh.shape["dp"], mesh.shape["tensor"]
    fine = Mesh(mesh.devices.reshape(dp // 2, 2, tensor), ("chip", "core", "tensor"))
    rows = ("chip", "core")
    every = ("chip", "core", "tensor")
    return jax.shard_map(
        per_device,
        mesh=fine,
        in_specs=(
            P(None, every),
            P(rows, "tensor"),
            P(rows, "tensor", None),
            P("tensor", rows),
            P(rows, None, "tensor", None),
            P(rows),
            P(rows, None, None),
            P(rows),
            P(rows, None),
            P(rows, "tensor"),
            P(rows, "tensor", None),
            P("tensor"),
        ),
        out_specs=(P(None, None, every), P(rows, None, None)),
        check_vma=False,
    )
```

time: 574 us -> 305 us (0.53)
  waiting for transfers between devices: 398 us -> 112 us
  starting transfers between devices: 8.73 us -> 56.8 us
  blocking collectives: 45.2 us -> 0 us
  matrix products: 59.9 us -> 73.1 us
  between operations: 14.5 us -> 1.34 us
  local copies, waits for them, and re-layouts: 40.1 us -> 50.9 us
    all_gather x4 -> x0, waiting for transfers between devices: 265 us -> none  [the longest x1 159 us: per_device(): lax.all_gather(critic_query_weight, 'dp', axis=0, tiled=True)]
    all_to_all x2 -> x13, waiting for transfers between devices: 2.32 us -> 107 us  [exchange(): return lax.all_to_all(pieces, axes, 0, 0, tiled=True)]
    reduce_scatter x3 -> x0, waiting for transfers between devices: 92.5 us -> none  [the longest x2 50.7 us: per_device(): summed = lax.psum_scatter(term, 'tensor', scatter_dimension=1, tiled=True)]
    all_to_all x2 -> x13, starting transfers between devices: 8.22 us -> 54.3 us  [exchange(): return lax.all_to_all(pieces, axes, 0, 0, tiled=True)]
    unnamed x9 -> x0, waiting for transfers between devices: 38.2 us -> none
    all_gather x2 -> x0, blocking collectives: 33.4 us -> none  [per_device(): gathered = lax.all_gather(current_state, 'tensor', axis=1, tiled=True)]
    unnamed x31 -> x26, local copies, waits for them, and re-layouts: 26.5 us -> 3.16 us
    dynamic_slice x0 -> x4, local copies, waits for them, and re-layouts: none -> 23.3 us  [pick(): return lax.dynamic_index_in_dim(x, index, axis, keepdims=False)]
  transfers between devices with their start and end apart: 10 -> 21, of which waited for: 9 -> 11; matrix products, arithmetic and copies ran while one was open for 7% -> 43% of each run, Pallas kernels for 0% -> 0%
where the time goes in v1:
time: 305 us; the launch traced here: 304 us
  waiting for transfers between devices  112 us (37%)
  matrix products  73.1 us (24%)
  starting transfers between devices  56.8 us (19%)
  local copies, waits for them, and re-layouts  50.9 us (17%)
  other arithmetic  9.8 us (3%)
    all_to_all x13, waiting for transfers between devices, exchange(): return lax.all_to_all(pieces, axes, 0, 0, tiled=True)  107 us
    dot_general x17, matrix products, dot(): return jnp.dot(a, b, preferred_element_type=F32)  55.5 us
    all_to_all x13, starting transfers between devices, exchange(): return lax.all_to_all(pieces, axes, 0, 0, tiled=True)  54.3 us
    dynamic_slice x4, local copies, waits for them, and re-layouts, pick(): return lax.dynamic_index_in_dim(x, index, axis, keepdims=False)  23.3 us
    slice x1, local copies, waits for them, and re-layouts, per_device(): cache_keys = kv_cache[..., :HEAD_DIM]  8.42 us
    reshape x1, local copies, waits for them, and re-layouts, per_device(): split = responses.reshape(tokens, chips, 2, width)  7.84 us
    dot_general x2, matrix products, cached_attention(): jnp.einsum('rkgd,rckd->rkgc', q, cache_keys, preferred_element_type=F32)  7.12 us
  transfers between devices with their start and end apart: 21, of which 11 were waited for; matrix products, arithmetic and copies ran while one was open for 43% of the time, Pallas kernels for 0%

profile of v1, /device:TPU:0, one launch (start us, length us, event | category | flops | bytes accessed | tf_op | source)
XLA Modules:
  0.0 303.7 jit_solution(4469428878458166266)
XLA Ops:
  4.2 4.1 %collective-permute-done = bf16[128,256]{1,0:T(8,128)(2,1)S(1)} collective-permute-done((bf16[128,256]{1,0:T(8,128)(2,1)S(1)}, bf16[128,256]{1,0:T(8,128)(2,1)S(1)}, u32[]{:S(2)}, u32[]{:S(2)}) %collective-permute-start) | collective-permute-done | bytes 65568 | tf_op jit(solution)/shard_map/ppermute | solution.py:21
  9.3 6.2 %all-to-all-start = ((bf16[4,128,512]{1,2,0:T(8,128)(2,1)}), bf16[4,128,512]{1,2,0:T(8,128)(2,1)S(1)}, u32[]{:S(2)}, u32[]{:S(2)}) async-start(bf16[4,128,512]{1,2,0:T(8,128)(2,1)} %broadcast_in_dim.110), calls=%async_computation | async-start | bytes 1048576 | tf_op jit(solution)/shard_map/all_to_all | solution.py:25
  15.6 8.4 %fusion.83 = (bf16[32,256,2,128]{3,2,1,0:T(2,128)(2,1)}, bf16[32,256,2,128]{3,2,1,0:T(2,128)(2,1)}) fusion(bf16[32,256,2,256]{3,2,1,0:T(2,128)(2,1)} %param.16), kind=kLoop, calls=%fused_computation.130 | loop fusion | bytes 16777216 | tf_op jit(solution)/shard_map/slice | solution.py:108
  24.0 7.8 %reshape.349 = bf16[256,4,2,1024]{3,2,1,0:T(2,128)(2,1)} reshape(bf16[16,16,8192]{2,1,0:T(8,128)(2,1)} %param.18) | data formatting | bytes 8388608 | tf_op jit(solution)/shard_map/reshape | solution.py:102
  39.4 3.7 %all-to-all-start.1 = ((bf16[4,32,2560]{2,1,0:T(8,128)(2,1)}), bf16[4,32,2560]{2,1,0:T(8,128)(2,1)S(1)}, u32[]{:S(2)}, u32[]{:S(2)}) async-start(bf16[4,32,2560]{2,1,0:T(8,128)(2,1)} %bitcast.8), calls=%async_computation.1 | async-start | bytes 1310720 | tf_op jit(solution)/shard_map/all_to_all | solution.py:25
  43.2 13.1 %constant_dynamic-slice_fusion.1 = (bf16[256,4,1,1024]{3,2,1,0:T(2,128)(2,1)}, bf16[256,4,1,1024]{3,2,1,0:T(2,128)(2,1)S(1)}) fusion(bf16[256,4,2,1024]{3,2,1,0:T(2,128)(2,1)} %reshape.349, s32[]{:T(128)S(6)} %select_n.63, s32[]{:T(128)S(6)} %select_n.62), kind=kLoop, calls=%fused_computation.122 | loop fusion | bytes 8388616 | tf_op jit(solution)/shard_map/jit(dynamic_index_in_dim)/dynamic_slice | solution.py:36
  59.9 4.5 %all-to-all-start.8 = ((bf16[4,256,1024]{2,1,0:T(8,128)(2,1)}), bf16[4,256,1024]{2,1,0:T(8,128)(2,1)}, u32[]{:S(2)}, u32[]{:S(2)}) async-start(bf16[4,256,1024]{2,1,0:T(8,128)(2,1)} %bitcast.194), calls=%async_computation.8 | async-start | bytes 4194304 | tf_op jit(solution)/shard_map/all_to_all | solution.py:25
  72.3 17.2 %all-to-all-done.8 = bf16[4,256,1024]{2,1,0:T(8,128)(2,1)} async-done(((bf16[4,256,1024]{2,1,0:T(8,128)(2,1)}), bf16[4,256,1024]{2,1,0:T(8,128)(2,1)}, u32[]{:S(2)}, u32[]{:S(2)}) %all-to-all-start.8) | async-done | bytes 2097184 | tf_op jit(solution)/shard_map/all_to_all | solution.py:25
  90.3 3.6 %all-to-all-start.2 = ((bf16[4,32,2048]{2,1,0:T(8,128)(2,1)}), bf16[4,32,2048]{2,1,0:T(8,128)(2,1)S(1)}, u32[]{:S(2)}, u32[]{:S(2)}) async-start(bf16[4,32,2048]{2,1,0:T(8,128)(2,1)} %broadcast_in_dim.113), calls=%async_computation.2 | async-start | bytes 1048576 | tf_op jit(solution)/shard_map/all_to_all | solution.py:25
  95.9 5.8 %copy.268 = bf16[256,4,1,1024]{3,0,2,1:T(8,128)(2,1)} copy(bf16[256,4,1,1024]{3,2,1,0:T(2,128)(2,1)} %get-tuple-element.6) | data formatting | bytes 4194304 | tf_op jit(solution)/shard_map/jit(dynamic_index_in_dim)/dynamic_slice | solution.py:36
  101.7 4.5 %all-to-all-start.9 = ((bf16[4,256,1024]{2,1,0:T(8,128)(2,1)}), bf16[4,256,1024]{2,1,0:T(8,128)(2,1)}, u32[]{:S(2)}, u32[]{:S(2)}) async-start(bf16[4,256,1024]{2,1,0:T(8,128)(2,1)} %bitcast.193), calls=%async_computation.9 | async-start | bytes 4194304 | tf_op jit(solution)/shard_map/all_to_all | solution.py:25
  113.1 18.5 %all-to-all-done.9 = bf16[4,256,1024]{2,1,0:T(8,128)(2,1)} async-done(((bf16[4,256,1024]{2,1,0:T(8,128)(2,1)}), bf16[4,256,1024]{2,1,0:T(8,128)(2,1)}, u32[]{:S(2)}, u32[]{:S(2)}) %all-to-all-start.9) | async-done | bytes 2097184 | tf_op jit(solution)/shard_map/all_to_all | solution.py:25
  131.6 4.8 %all-to-all-start.3 = ((bf16[4,128,512]{2,1,0:T(8,128)(2,1)}), bf16[4,128,512]{2,1,0:T(8,128)(2,1)S(1)}, u32[]{:S(2)}, u32[]{:S(2)}) async-start(bf16[4,128,512]{2,1,0:T(8,128)(2,1)} %maximum_bitcast_fusion), calls=%async_computation.3 | async-start | bytes 1048576 | tf_op jit(solution)/shard_map/all_to_all | solution.py:25
  139.5 4.1 %add_convert_fusion.2 = bf16[1024,512]{1,0:T(8,128)(2,1)} fusion(f32[1024,512]{1,0:T(8,128)S(1)} %fusion.99, bf16[1024,1024]{1,0:T(8,128)(2,1)} %bitcast.42, bf16[1024,512]{1,0:T(8,128)(2,1)} %collective-permute-done.6), kind=kOutput, calls=%fused_computation.20 | convolution fusion | flops 1074790400 | bytes 6291456 | tf_op jit(solution)/shard_map/dot_general | solution.py:17
  143.6 6.6 %all-to-all-done.3 = bf16[4,128,512]{2,1,0:T(8,128)(2,1)S(1)} async-done(((bf16[4,128,512]{2,1,0:T(8,128)(2,1)}), bf16[4,128,512]{2,1,0:T(8,128)(2,1)S(1)}, u32[]{:S(2)}, u32[]{:S(2)}) %all-to-all-start.3) | async-done | bytes 524320 | tf_op jit(solution)/shard_map/all_to_all | solution.py:25
  154.8 10.6 %fusion.100 = f32[1024,2048]{1,0:T(8,128)} fusion(bf16[1024,1024]{1,0:T(8,128)(2,1)} %bitcast.39, bf16[1024,2048]{1,0:T(8,128)(2,1)} %param.21), kind=kOutput, calls=%fused_computation.145 | convolution fusion | flops 4294967296 | bytes 14680064 | tf_op jit(solution)/shard_map/dot_general | solution.py:17
  179.9 5.6 %all-to-all-done.10 = bf16[4,256,512]{2,1,0:T(8,128)(2,1)S(1)} async-done(((bf16[4,256,512]{2,1,0:T(8,128)(2,1)}), bf16[4,256,512]{2,1,0:T(8,128)(2,1)S(1)}, u32[]{:S(2)}, u32[]{:S(2)}) %all-to-all-start.10) | async-done | bytes 1048608 | tf_op jit(solution)/shard_map/all_to_all | solution.py:25
  185.5 3.7 %all-to-all-start.5 = ((bf16[4,32,2560]{2,1,0:T(8,128)(2,1)}), bf16[4,32,2560]{2,1,0:T(8,128)(2,1)S(1)}, u32[]{:S(2)}, u32[]{:S(2)}) async-start(bf16[4,32,2560]{2,1,0:T(8,128)(2,1)} %bitcast.28), calls=%async_computation.5 | async-start | bytes 1310720 | tf_op jit(solution)/shard_map/all_to_all | solution.py:25
  189.2 11.8 %add_convert_fusion = bf16[1024,2048]{1,0:T(8,128)(2,1)} fusion(f32[1024,2048]{1,0:T(8,128)} %fusion.100, bf16[1024,1024]{1,0:T(8,128)(2,1)} %bitcast.42, bf16[1024,2048]{1,0:T(8,128)(2,1)} %collective-permute-done.7), kind=kOutput, calls=%fused_computation.1 | convolution fusion | flops 4299161600 | bytes 18874368 | tf_op jit(solution)/shard_map/dot_general | solution.py:17
  201.0 5.0 %all-to-all-start.11 = ((bf16[4,256,2048]{2,1,0:T(8,128)(2,1)}), bf16[4,256,2048]{2,1,0:T(8,128)(2,1)}, u32[]{:S(2)}, u32[]{:S(2)}) async-start(bf16[4,256,2048]{2,1,0:T(8,128)(2,1)} %bitcast.207), calls=%async_computation.11 | async-start | bytes 8388608 | tf_op jit(solution)/shard_map/all_to_all | solution.py:25
  212.3 40.7 %all-to-all-done.11 = bf16[4,256,2048]{2,1,0:T(8,128)(2,1)} async-done(((bf16[4,256,2048]{2,1,0:T(8,128)(2,1)}), bf16[4,256,2048]{2,1,0:T(8,128)(2,1)}, u32[]{:S(2)}, u32[]{:S(2)}) %all-to-all-start.11) | async-done | bytes 4194336 | tf_op jit(solution)/shard_map/all_to_all | solution.py:25
  260.4 3.9 %fusion.92 = (f32[16,2,8,16]{3,2,1,0:T(8,128)S(1)}, f32[16,2,8,16,16]{3,4,2,1,0:T(8,128)}) fusion(pred[16,16,16]{1,2,0:T(8,128)(4,1)S(1)} %fusion.56, bf16[16,16,2,8,128]{4,3,2,1,0:T(8,128)(2,1)S(1)} %bitcast.223, bf16[16,16,2,128]{3,2,1,0:T(2,128)(2,1)S(1)} %get-tuple-element.13), kind=kOutput, calls=%fused_computation.139 | convolution fusion | flops 17039376 | bytes 1462272 | tf_op jit(solution)/shard_map/sub | solution.py:65
  282.1 4.3 %all-to-all-start.7 = ((bf16[4,128,512]{2,1,0:T(8,128)(2,1)}), bf16[4,128,512]{2,1,0:T(8,128)(2,1)S(1)}, u32[]{:S(2)}, u32[]{:S(2)}) async-start(bf16[4,128,512]{2,1,0:T(8,128)(2,1)} %maximum_bitcast_fusion.1), calls=%async_computation.7 | async-start | bytes 1048576 | tf_op jit(solution)/shard_map/all_to_all | solution.py:25
  287.0 14.2 %all-to-all-done.7 = bf16[4,128,512]{2,1,0:T(8,128)(2,1)S(1)} async-done(((bf16[4,128,512]{2,1,0:T(8,128)(2,1)}), bf16[4,128,512]{2,1,0:T(8,128)(2,1)S(1)}, u32[]{:S(2)}, u32[]{:S(2)}) %all-to-all-start.7) | async-done | bytes 524320 | tf_op jit(solution)/shard_map/all_to_all | solution.py:25
  (141 shorter events, 89.6 us)
Async XLA Ops:
  0.6 34.9 %collective-permute-start.1 = (bf16[1024,2048]{1,0:T(8,128)(2,1)}, bf16[1024,2048]{1,0:T(8,128)(2,1)}, u32[]{:S(2)}, u32[]{:S(2)}) collective-permute-start(bf16[1024,2048]{1,0:T(8,128)(2,1)} %param.13), channel_id=1, source_target_pairs={{0,4},{4,0},{1,5},{5,1},{2,6},{6,2},{3,7},{7,3},{8,12},{12,8},{9,1... | collective-permute-start | bytes 12582920 | tf_op jit(solution)/shard_map/ppermute | solution.py:21
  2.1 6.2 %collective-permute-start = (bf16[128,256]{1,0:T(8,128)(2,1)S(1)}, bf16[128,256]{1,0:T(8,128)(2,1)S(1)}, u32[]{:S(2)}, u32[]{:S(2)}) collective-permute-start(bf16[128,256]{1,0:T(8,128)(2,1)S(1)} %bitcast.247), channel_id=1, source_target_pairs={{0,4},{4,0},{1,5},{5,1},{2,6},{6,2},{3,7},{7,3},{8,12},{12,8},{9,1... | collective-permute-start | bytes 196616 | tf_op jit(solution)/shard_map/ppermute | solution.py:21
  3.6 31.5 %collective-permute-start.2 = (bf16[1024,512]{1,0:T(8,128)(2,1)S(1)}, bf16[1024,512]{1,0:T(8,128)(2,1)S(1)}, u32[]{:S(2)}, u32[]{:S(2)}) collective-permute-start(bf16[1024,512]{1,0:T(8,128)(2,1)S(1)} %bitcast.200), channel_id=1, source_target_pairs={{0,4},{4,0},{1,5},{5,1},{2,6},{6,2},{3,7},{7,3},{8,12},{12,8},{9,1... | collective-permute-start | bytes 3145736 | tf_op jit(solution)/shard_map/ppermute | solution.py:21
  4.2 105.2 %collective-permute-start.3 = (bf16[2048,1024]{1,0:T(8,128)(2,1)}, bf16[2048,1024]{1,0:T(8,128)(2,1)}, u32[]{:S(2)}, u32[]{:S(2)}) collective-permute-start(bf16[2048,1024]{1,0:T(8,128)(2,1)} %param.15), channel_id=1, source_target_pairs={{0,4},{4,0},{1,5},{5,1},{2,6},{6,2},{3,7},{7,3},{8,12},{12,8},{9,1... | collective-permute-start | bytes 12582920 | tf_op jit(solution)/shard_map/ppermute | solution.py:21
  9.3 22.5 %all-to-all-start = ((bf16[4,128,512]{1,2,0:T(8,128)(2,1)}), bf16[4,128,512]{1,2,0:T(8,128)(2,1)S(1)}, u32[]{:S(2)}, u32[]{:S(2)}) async-start(bf16[4,128,512]{1,2,0:T(8,128)(2,1)} %broadcast_in_dim.110), calls=%async_computation | async-start | bytes 1048576 | tf_op jit(solution)/shard_map/all_to_all | solution.py:25
  39.4 20.5 %all-to-all-start.1 = ((bf16[4,32,2560]{2,1,0:T(8,128)(2,1)}), bf16[4,32,2560]{2,1,0:T(8,128)(2,1)S(1)}, u32[]{:S(2)}, u32[]{:S(2)}) async-start(bf16[4,32,2560]{2,1,0:T(8,128)(2,1)} %bitcast.8), calls=%async_computation.1 | async-start | bytes 1310720 | tf_op jit(solution)/shard_map/all_to_all | solution.py:25
  59.9 29.5 %all-to-all-start.8 = ((bf16[4,256,1024]{2,1,0:T(8,128)(2,1)}), bf16[4,256,1024]{2,1,0:T(8,128)(2,1)}, u32[]{:S(2)}, u32[]{:S(2)}) async-start(bf16[4,256,1024]{2,1,0:T(8,128)(2,1)} %bitcast.194), calls=%async_computation.8 | async-start | bytes 4194304 | tf_op jit(solution)/shard_map/all_to_all | solution.py:25
  69.2 24.9 %copy-start.3 = (bf16[1024,2,256]{2,1,0:T(2,128)(2,1)S(1)}, bf16[1024,2,256]{2,1,0:T(2,128)(2,1)}, u32[]{:S(2)}) copy-start(bf16[1024,2,256]{2,1,0:T(2,128)(2,1)} %param.22) | copy-start | bytes 3145732
  90.3 11.4 %all-to-all-start.2 = ((bf16[4,32,2048]{2,1,0:T(8,128)(2,1)}), bf16[4,32,2048]{2,1,0:T(8,128)(2,1)S(1)}, u32[]{:S(2)}, u32[]{:S(2)}) async-start(bf16[4,32,2048]{2,1,0:T(8,128)(2,1)} %broadcast_in_dim.113), calls=%async_computation.2 | async-start | bytes 1048576 | tf_op jit(solution)/shard_map/all_to_all | solution.py:25
  94.0 95.2 %collective-permute-start.7 = (bf16[1024,2048]{1,0:T(8,128)(2,1)}, bf16[1024,2048]{1,0:T(8,128)(2,1)}, u32[]{:S(2)}, u32[]{:S(2)}) collective-permute-start(bf16[1024,2048]{1,0:T(8,128)(2,1)} %param.21), channel_id=1, source_target_pairs={{0,4},{4,0},{1,5},{5,1},{2,6},{6,2},{3,7},{7,3},{8,12},{12,8},{9,1... | collective-permute-start | bytes 12582920 | tf_op jit(solution)/shard_map/ppermute | solution.py:21
  94.1 7.5 %copy-start.6 = (s32[16,1]{0,1:T(1,128)S(1)}, s32[16,1]{0,1:T(1,128)}, u32[]{:S(2)}) copy-start(s32[16,1]{0,1:T(1,128)} %param.20) | copy-start | bytes 196
  95.4 44.1 %collective-permute-start.6 = (bf16[1024,512]{1,0:T(8,128)(2,1)}, bf16[1024,512]{1,0:T(8,128)(2,1)}, u32[]{:S(2)}, u32[]{:S(2)}) collective-permute-start(bf16[1024,512]{1,0:T(8,128)(2,1)} %bitcast.85), channel_id=1, source_target_pairs={{0,4},{4,0},{1,5},{5,1},{2,6},{6,2},{3,7},{7,3},{8,12},{12,8},{9,1... | collective-permute-start | bytes 3145736 | tf_op jit(solution)/shard_map/ppermute | solution.py:21
  101.7 29.9 %all-to-all-start.9 = ((bf16[4,256,1024]{2,1,0:T(8,128)(2,1)}), bf16[4,256,1024]{2,1,0:T(8,128)(2,1)}, u32[]{:S(2)}, u32[]{:S(2)}) async-start(bf16[4,256,1024]{2,1,0:T(8,128)(2,1)} %bitcast.193), calls=%async_computation.9 | async-start | bytes 4194304 | tf_op jit(solution)/shard_map/all_to_all | solution.py:25
  131.6 18.6 %all-to-all-start.3 = ((bf16[4,128,512]{2,1,0:T(8,128)(2,1)}), bf16[4,128,512]{2,1,0:T(8,128)(2,1)S(1)}, u32[]{:S(2)}, u32[]{:S(2)}) async-start(bf16[4,128,512]{2,1,0:T(8,128)(2,1)} %maximum_bitcast_fusion), calls=%async_computation.3 | async-start | bytes 1048576 | tf_op jit(solution)/shard_map/all_to_all | solution.py:25
  151.4 17.5 %all-to-all-start.4 = ((bf16[4,128,512]{1,2,0:T(8,128)(2,1)}), bf16[4,128,512]{1,2,0:T(8,128)(2,1)S(1)}, u32[]{:S(2)}, u32[]{:S(2)}) async-start(bf16[4,128,512]{1,2,0:T(8,128)(2,1)} %broadcast_in_dim.115), calls=%async_computation.4 | async-start | bytes 1048576 | tf_op jit(solution)/shard_map/all_to_all | solution.py:25
  168.8 16.7 %all-to-all-start.10 = ((bf16[4,256,512]{2,1,0:T(8,128)(2,1)}), bf16[4,256,512]{2,1,0:T(8,128)(2,1)S(1)}, u32[]{:S(2)}, u32[]{:S(2)}) async-start(bf16[4,256,512]{2,1,0:T(8,128)(2,1)} %bitcast.222), calls=%async_computation.10 | async-start | bytes 2097152 | tf_op jit(solution)/shard_map/all_to_all | solution.py:25
  185.5 15.5 %all-to-all-start.5 = ((bf16[4,32,2560]{2,1,0:T(8,128)(2,1)}), bf16[4,32,2560]{2,1,0:T(8,128)(2,1)S(1)}, u32[]{:S(2)}, u32[]{:S(2)}) async-start(bf16[4,32,2560]{2,1,0:T(8,128)(2,1)} %bitcast.28), calls=%async_computation.5 | async-start | bytes 1310720 | tf_op jit(solution)/shard_map/all_to_all | solution.py:25
  201.0 5.1 %copy-start.5 = (s32[16]{0:T(128)S(1)}, s32[16]{0:T(128)}, u32[]{:S(2)}) copy-start(s32[16]{0:T(128)} %param.19) | copy-start | bytes 196
  201.0 51.9 %all-to-all-start.11 = ((bf16[4,256,2048]{2,1,0:T(8,128)(2,1)}), bf16[4,256,2048]{2,1,0:T(8,128)(2,1)}, u32[]{:S(2)}, u32[]{:S(2)}) async-start(bf16[4,256,2048]{2,1,0:T(8,128)(2,1)} %bitcast.207), calls=%async_computation.11 | async-start | bytes 8388608 | tf_op jit(solution)/shard_map/all_to_all | solution.py:25
  253.8 16.9 %all-to-all-start.6 = ((bf16[4,32,2048]{2,1,0:T(8,128)(2,1)}), bf16[4,32,2048]{2,1,0:T(8,128)(2,1)S(1)}, u32[]{:S(2)}, u32[]{:S(2)}) async-start(bf16[4,32,2048]{2,1,0:T(8,128)(2,1)} %broadcast_in_dim.117), calls=%async_computation.6 | async-start | bytes 1048576 | tf_op jit(solution)/shard_map/all_to_all | solution.py:25
  271.4 10.7 %all-to-all-start.12 = ((f32[32,2,16]{2,1,0:T(2,128)}), f32[32,2,16]{2,1,0:T(2,128)S(1)}, u32[]{:S(2)}, u32[]{:S(2)}) async-start(f32[32,2,16]{2,1,0:T(2,128)} %bitcast.54), calls=%async_computation.12 | async-start | bytes 65536 | tf_op jit(solution)/shard_map/all_to_all | solution.py:25
  282.1 19.1 %all-to-all-start.7 = ((bf16[4,128,512]{2,1,0:T(8,128)(2,1)}), bf16[4,128,512]{2,1,0:T(8,128)(2,1)S(1)}, u32[]{:S(2)}, u32[]{:S(2)}) async-start(bf16[4,128,512]{2,1,0:T(8,128)(2,1)} %maximum_bitcast_fusion.1), calls=%async_computation.7 | async-start | bytes 1048576 | tf_op jit(solution)/shard_map/all_to_all | solution.py:25
  301.4 1.3 collective-permute-start.5
  301.5 1.5 collective-permute-start.4
  (5 other events, 20.9 us)

commit v2 on v1

v2 whole, which is shorter than its diff:
```python
import jax
import jax.numpy as jnp
from jax import lax
from jax.experimental import pallas as pl
from jax.experimental.pallas import tpu as pltpu
from jax.sharding import Mesh, PartitionSpec as P

QUERY_HEADS = 64
KEY_HEADS = 8
HEAD_DIM = 128
STEPS = 2
CAPR = 2
F32 = jnp.float32
BF16 = jnp.bfloat16
SCALE = HEAD_DIM ** (-0.5)


def dot(a, b):
    return jnp.dot(a, b, preferred_element_type=F32)


def swap(x):
    return lax.ppermute(x, "core", [(0, 1), (1, 0)])


def flip(x, axes, s, count):
    return lax.ppermute(x, axes, [(i, i ^ s) for i in range(count)])


def exchange(pieces, axes):
    return lax.all_to_all(pieces, axes, 0, 0, tiled=True)


def add_up(pieces):
    total = pieces[0].astype(F32)
    for i in range(1, pieces.shape[0]):
        total = total + pieces[i].astype(F32)
    return total


def pick(x, index, axis):
    return lax.dynamic_index_in_dim(x, index, axis, keepdims=False)


def two_sided(x_mine, x_other, specs, wide, narrow, rows, depth, steps):
    n_wide, n_narrow = wide[0].shape[1], narrow[0].shape[1]

    def kernel(xm, xo, a0, a1, b0, b1, out, acc):
        k = pl.program_id(0)
        left = xm[...].reshape(rows, depth)
        right = xo[...].reshape(rows, depth)
        first = dot(left, a0[...]) + dot(right, a1[...])
        second = dot(left, b0[...]) + dot(right, b1[...])

        @pl.when(k == 0)
        def _():
            acc[:, :n_wide] = first
            acc[:, n_wide:] = second

        @pl.when(k > 0)
        def _():
            acc[:, :n_wide] += first
            acc[:, n_wide:] += second

        @pl.when(k == steps - 1)
        def _():
            out[...] = acc[...].astype(BF16)

    return pl.pallas_call(
        kernel,
        grid=(steps,),
        in_specs=list(specs)
        + [pl.BlockSpec((depth, n_wide), lambda k: (k, 0))] * 2
        + [pl.BlockSpec((depth, n_narrow), lambda k: (k, 0))] * 2,
        out_specs=pl.BlockSpec((rows, n_wide + n_narrow), lambda k: (0, 0)),
        out_shape=jax.ShapeDtypeStruct((rows, n_wide + n_narrow), BF16),
        scratch_shapes=[pltpu.VMEM((rows, n_wide + n_narrow), F32)],
        name="two_sided",
    )(x_mine, x_other, wide[0], wide[1], narrow[0], narrow[1])


def halves_product(x, wide, narrow):
    rows, width = x.shape[0], wide[0].shape[0]
    depth = min(256, width)
    steps = width // depth
    specs = (
        pl.BlockSpec((rows, depth), lambda k: (0, k)),
        pl.BlockSpec((rows, depth), lambda k: (0, steps + k)),
    )
    return two_sided(x, x, specs, wide, narrow, rows, depth, steps)


def pieces_product(x, wide, narrow):
    zs, rows, both = x.shape
    piece = both // 2
    if piece % 128:
        flat = x.reshape(zs, rows, 2, piece).transpose(1, 2, 0, 3).reshape(rows, zs * both)
        return halves_product(flat, wide, narrow)
    specs = (
        pl.BlockSpec((1, rows, piece), lambda k: (k, 0, 0)),
        pl.BlockSpec((1, rows, piece), lambda k: (k, 0, 1)),
    )
    return two_sided(x, x, specs, wide, narrow, rows, piece, zs)


def output_terms(x, weights, zs):
    rows, depth = x.shape
    piece = weights[0].shape[1] // zs
    if piece % 128:
        mine = dot(x, weights[0]).astype(BF16).reshape(rows, zs, piece)
        other = dot(x, weights[1]).astype(BF16).reshape(rows, zs, piece)
        return jnp.concatenate([mine, other], 2).transpose(1, 0, 2)

    def kernel(xr, a, b, out):
        out[0, :, :piece] = dot(xr[...], a[...]).astype(BF16)
        out[0, :, piece:] = dot(xr[...], b[...]).astype(BF16)

    return pl.pallas_call(
        kernel,
        grid=(zs,),
        in_specs=[pl.BlockSpec((rows, depth), lambda t: (0, 0))]
        + [pl.BlockSpec((depth, piece), lambda t: (0, t))] * 2,
        out_specs=pl.BlockSpec((1, rows, 2 * piece), lambda t: (t, 0, 0)),
        out_shape=jax.ShapeDtypeStruct((zs, rows, 2 * piece), BF16),
        name="output_terms",
    )(x, weights[0], weights[1])


def cached_attention(q, cache_keys, cache_values, cache_mask, new_keys, new_values, step):
    old_scores = jnp.einsum("rkgd,rckd->rkgc", q, cache_keys, preferred_element_type=F32) * SCALE
    old_scores = jnp.where(cache_mask[:, None, None, :], old_scores, -1e30)
    new_scores = jnp.einsum("rkgd,trkd->rkgt", q, new_keys, preferred_element_type=F32) * SCALE
    known = lax.broadcasted_iota(jnp.int32, new_scores.shape, 3) <= step
    new_scores = jnp.where(known, new_scores, -1e30)
    top = jnp.maximum(jnp.max(old_scores, -1), jnp.max(new_scores, -1))
    old_exp = jnp.exp(old_scores - top[..., None])
    new_exp = jnp.exp(new_scores - top[..., None])
    total = jnp.sum(old_exp, -1) + jnp.sum(new_exp, -1)
    old_weights = (old_exp / total[..., None]).astype(BF16)
    new_weights = (new_exp / total[..., None]).astype(BF16)
    mixed = jnp.einsum("rkgc,rckd->rkgd", old_weights, cache_values, preferred_element_type=F32)
    mixed = mixed + jnp.einsum("rkgt,trkd->rkgd", new_weights, new_values, preferred_element_type=F32)
    return mixed.astype(BF16)


def critic_partials(queries, pairs, lengths, score_weight):
    rows, tok_len = queries.shape[:2]
    scores = (
        jnp.einsum("stkgd,sukd->skgtu", queries, pairs[..., :HEAD_DIM], preferred_element_type=F32)
        * SCALE
    )
    later = lax.broadcasted_iota(jnp.int32, (tok_len, tok_len), 1)
    earlier = lax.broadcasted_iota(jnp.int32, (tok_len, tok_len), 0)
    allowed = (later[None] <= earlier[None]) & (later[None] < lengths[:, None, None])
    scores = jnp.where(allowed[:, None, None], scores, -1e30)
    top = jnp.max(scores, -1, keepdims=True)
    expo = jnp.exp(scores - top)
    weights = (expo / jnp.sum(expo, -1, keepdims=True)).astype(BF16)
    mixed = jnp.einsum("skgtu,sukd->stkgd", weights, pairs[..., HEAD_DIM:], preferred_element_type=F32)
    mixed = mixed.astype(BF16).reshape(rows, tok_len, -1)
    partial_values = dot(mixed, score_weight)
    valid = lax.broadcasted_iota(jnp.int32, (rows, tok_len), 1) < lengths[:, None]
    return jnp.where(valid, partial_values, 0.0)


def by_flip(x, me):
    n = x.shape[0]
    at = lax.broadcasted_iota(jnp.int32, (n, n), 0) ^ me
    chosen = at == lax.broadcasted_iota(jnp.int32, (n, n), 1)
    return jnp.sum(jnp.where(chosen[:, :, None, None], x[None], 0.0), 1)


def per_device(
    layer_inputs,
    policy_query_weight,
    policy_key_value,
    policy_out,
    kv_cache,
    prefix_len,
    responses,
    response_len,
    assign,
    critic_query_weight,
    critic_key_value,
    score_weight,
):
    chips = lax.axis_size("chip")
    zs = lax.axis_size("tensor")
    core = lax.axis_index("core")
    chip = lax.axis_index("chip")
    odd = lax.axis_index("tensor") & 1
    shards = chips * 2
    rows = kv_cache.shape[0]
    heads = kv_cache.shape[2]
    group = QUERY_HEADS // KEY_HEADS
    width = policy_query_weight.shape[0]
    q_width = policy_query_weight.shape[1]
    piece = layer_inputs.shape[1]
    half = chips * rows
    src_rows, tok_len, model_width = responses.shape
    tokens = src_rows * tok_len
    flat = responses.reshape(tokens, model_width)

    def features(s, part):
        start = (odd ^ part) * (tokens // 2)
        column = (chip ^ s) * (2 * width)
        mine = lax.dynamic_slice(flat, (start, column + core * width), (tokens // 2, width))
        other = lax.dynamic_slice(flat, (start, column + (1 - core) * width), (tokens // 2, width))
        return jnp.concatenate([mine, other], 1)

    def turned(x):
        return jnp.where(odd == 0, x, jnp.roll(x, src_rows // 2, 0))

    pk = policy_key_value.reshape(width, -1)
    ck = critic_key_value.reshape(width, -1)
    by_core = layer_inputs.reshape(chips, 2, rows, piece)
    kept = pick(by_core, core, 1).reshape(half, piece)
    got = swap(pick(by_core, 1 - core, 1).reshape(half, piece))
    state = jnp.concatenate([kept, got], 1)
    wq = (policy_query_weight, swap(policy_query_weight))
    wk = (pk, swap(pk))
    wo = (policy_out, swap(policy_out))
    cq = (critic_query_weight, swap(critic_query_weight))
    ck = (ck, swap(ck))

    near = {s: flip(features(s, 0), "chip", s, chips) for s in range(1, chips)}
    far = {s: flip(near[s], "tensor", 1, zs) for s in near}
    cache_keys = kv_cache[..., :HEAD_DIM]
    cache_values = kv_cache[..., HEAD_DIM:]
    cache_mask = lax.broadcasted_iota(jnp.int32, (rows, kv_cache.shape[1]), 1) < prefix_len[:, None]

    def spread_out(state):
        return exchange(jnp.broadcast_to(state[None], (zs, half, 2 * piece)), "tensor")

    fresh = []

    def attend(projected, step):
        q = projected[:, :q_width].reshape(rows, heads, group, HEAD_DIM)
        fresh.append(projected[:, q_width:].reshape(rows, heads, 2 * HEAD_DIM))
        fresh_all = jnp.stack(fresh + [fresh[0]] * (STEPS - len(fresh)))
        return cached_attention(
            q,
            cache_keys,
            cache_values,
            cache_mask,
            fresh_all[..., :HEAD_DIM],
            fresh_all[..., HEAD_DIM:],
            step,
        ).reshape(rows, q_width)

    def gather_rows(attended):
        copies = jnp.broadcast_to(attended[None], (chips, rows, q_width))
        return exchange(copies, "chip").reshape(half, q_width)

    def own_features(state):
        back = swap(state[:, piece:]).reshape(chips, 1, rows, piece)
        own = state[:, :piece].reshape(chips, 1, rows, piece)
        both = jnp.where(core == 0, jnp.concatenate([own, back], 1), jnp.concatenate([back, own], 1))
        return both.reshape(shards * rows, piece)

    part = pieces_product(spread_out(state), wq, wk)
    arrived = exchange(part.reshape(chips, rows, -1), "chip")
    partials = {0: halves_product(jnp.concatenate([features(0, 0), features(0, 1)], 0), cq, ck)}
    attended = attend(add_up(arrived).astype(BF16), 0)
    gathered = gather_rows(attended)
    ready = {}
    for s in near:
        ready[s] = halves_product(jnp.concatenate([near[s], far[s]], 0), cq, ck)
    for s in near:
        partials[s] = flip(ready[s], "chip", s, chips)
    summed = add_up(exchange(output_terms(gathered, wo, zs), "tensor"))
    state = (state.astype(F32) + summed).astype(BF16)
    spread = spread_out(state)
    outputs = [own_features(state)]
    part = pieces_product(spread, wq, wk)
    arrived = exchange(part.reshape(chips, rows, -1), "chip")
    attended = attend(add_up(arrived).astype(BF16), 1)
    gathered = gather_rows(attended)

    sums = 0.0
    for s in range(chips):
        sums = sums + partials[s].astype(F32)
    sums = sums.astype(BF16)
    partial_values = critic_partials(
        sums[:, :q_width].reshape(src_rows, tok_len, heads, group, HEAD_DIM),
        sums[:, q_width:].reshape(src_rows, tok_len, heads, 2 * HEAD_DIM),
        turned(response_len),
        score_weight,
    )
    dest = assign[:, 0]
    onehot = (dest[:, None] == lax.broadcasted_iota(jnp.int32, (1, shards), 1)).astype(jnp.int32)
    rank = jnp.sum((jnp.cumsum(onehot, 0) - onehot) * onehot, 1)
    slot = turned(dest * CAPR + rank)
    chosen = lax.broadcasted_iota(jnp.int32, (shards * CAPR, src_rows), 0) == slot[None, :]
    packed = jnp.sum(jnp.where(chosen[:, :, None], partial_values[None], 0.0), 1)
    total = packed
    for s in range(1, zs):
        total = total + flip(packed, "tensor", s, zs)
    me = chip * 2 + core
    leaving = by_flip(total.reshape(shards, CAPR, tok_len), me)
    arriving = [leaving[0]]
    for s in range(1, shards):
        arriving.append(flip(leaving[s], ("chip", "core"), s, shards))
    values = by_flip(jnp.stack(arriving), me)

    summed = add_up(exchange(output_terms(gathered, wo, zs), "tensor"))
    state = (state.astype(F32) + summed).astype(BF16)
    outputs.append(own_features(state))
    return jnp.stack(outputs), values.reshape(1, shards * CAPR, tok_len)


def solution(mesh):
    dp, tensor = mesh.shape["dp"], mesh.shape["tensor"]
    fine = Mesh(mesh.devices.reshape(dp // 2, 2, tensor), ("chip", "core", "tensor"))
    rows = ("chip", "core")
    every = ("chip", "core", "tensor")

    return jax.shard_map(
        per_device,
        mesh=fine,
        in_specs=(
            P(None, every),
            P(rows, "tensor"),
            P(rows, "tensor", None),
            P("tensor", rows),
            P(rows, None, "tensor", None),
            P(rows),
            P(rows, None, None),
            P(rows),
            P(rows, None),
            P(rows, "tensor"),
            P(rows, "tensor", None),
            P("tensor"),
        ),
        out_specs=(P(None, None, every), P(rows, None, None)),
        check_vma=False,
    )
```

time: 305 us -> 264 us (0.87)
  Pallas kernels: 0 us -> 57 us
  matrix products: 73.1 us -> 17.2 us
  local copies, waits for them, and re-layouts: 50.9 us -> 24.5 us
  waiting for transfers between devices: 112 us -> 88.8 us
  other arithmetic: 9.8 us -> 16.5 us
    all_to_all x13 -> x8, waiting for transfers between devices: 107 us -> 49.6 us  [exchange(): return lax.all_to_all(pieces, axes, 0, 0, tiled=True)]
    pallas_call x0 -> x8, Pallas kernels: none -> 57 us  [the longest x6 45.5 us: two_sided(): pl.pallas_call(kernel, grid=(steps,), in_specs=list(specs) + [pl.BlockSpe...]
    dot_general x17 -> x1, matrix products: 55.5 us -> 1.32 us  [dot(): return jnp.dot(a, b, preferred_element_type=F32)]
    ppermute x0 -> x19, waiting for transfers between devices: none -> 38.9 us  [flip(): return lax.ppermute(x, axes, [(i, i ^ s) for i in range(count)])]
    ppermute x0 -> x19, starting transfers between devices: none -> 25.1 us  [flip(): return lax.ppermute(x, axes, [(i, i ^ s) for i in range(count)])]
    all_to_all x13 -> x8, starting transfers between devices: 54.3 us -> 29.6 us  [exchange(): return lax.all_to_all(pieces, axes, 0, 0, tiled=True)]
    dynamic_slice x4 -> x1, local copies, waits for them, and re-layouts: 23.3 us -> 0.89 us  [pick(): return lax.dynamic_index_in_dim(x, index, axis, keepdims=False)]
    reshape x4 -> x1, local copies, waits for them, and re-layouts: 7.92 us -> 0.07 us  [per_device(): sums[:, q_width:].reshape(src_rows, tok_len, heads, 2 * HEAD_DIM)]
  transfers between devices with their start and end apart: 21 -> 35, of which waited for: 11 -> 12; matrix products, arithmetic and copies ran while one was open for 43% -> 20% of each run, Pallas kernels for 0% -> 19%
where the time goes in v2:
time: 264 us; the launch traced here: 262 us
  waiting for transfers between devices  88.8 us (34%)
  starting transfers between devices  57 us (22%)
  Pallas kernels  57 us (22%)
  local copies, waits for them, and re-layouts  24.5 us (9%)
  matrix products  17.2 us (7%)
  other arithmetic  16.5 us (6%)
    all_to_all x8, waiting for transfers between devices, exchange(): return lax.all_to_all(pieces, axes, 0, 0, tiled=True)  49.6 us
    pallas_call x6, Pallas kernels, two_sided(): pl.pallas_call(kernel, grid=(steps,), in_specs=list(specs) + [pl.BlockSpe...  45.5 us
    ppermute x19, waiting for transfers between devices, flip(): return lax.ppermute(x, axes, [(i, i ^ s) for i in range(count)])  38.9 us
    all_to_all x8, starting transfers between devices, exchange(): return lax.all_to_all(pieces, axes, 0, 0, tiled=True)  29.6 us
    ppermute x19, starting transfers between devices, flip(): return lax.ppermute(x, axes, [(i, i ^ s) for i in range(count)])  25.1 us
    pallas_call x2, Pallas kernels, output_terms(): pl.pallas_call(kernel, grid=(zs,), in_specs=[pl.BlockSpec((rows, depth),...  11.5 us
    slice x1, local copies, waits for them, and re-layouts, per_device(): cache_values = kv_cache[..., HEAD_DIM:]  8.41 us
    unnamed x61, local copies, waits for them, and re-layouts  7.71 us
  transfers between devices with their start and end apart: 35, of which 12 were waited for; matrix products, arithmetic and copies ran while one was open for 20% of the time, Pallas kernels for 19%

profile of v2, /device:TPU:0, one launch (start us, length us, event | category | flops | bytes accessed | tf_op | source)
XLA Modules:
  0.0 262.4 jit_solution(17808485321306104903)
XLA Ops:
  7.0 3.8 %collective-permute-start.14 = (bf16[128,2048]{1,0:T(8,128)(2,1)S(1)}, bf16[128,2048]{1,0:T(8,128)(2,1)}, u32[]{:S(2)}, u32[]{:S(2)}) collective-permute-start(bf16[128,2048]{1,0:T(8,128)(2,1)S(1)} %pad_maximum_fusion.5), channel_id=1, source_target_pairs={{0,24},{8,16},{16,8},{24,0},{1,25},{9,17},{17,9},{25,1},{2,26},{10... | collective-permute-start | bytes 1572872 | tf_op jit(solution)/shard_map/ppermute | solution.py:27
  12.1 8.4 %fusion.83 = (bf16[32,256,2,128]{3,2,1,0:T(2,128)(2,1)}, bf16[32,256,2,128]{3,2,1,0:T(2,128)(2,1)}) fusion(bf16[32,256,2,256]{3,2,1,0:T(2,128)(2,1)} %param.16), kind=kLoop, calls=%fused_computation.137 | loop fusion | bytes 16777216 | tf_op jit(solution)/shard_map/slice | solution.py:229
  25.0 10.2 %collective-permute-done.11 = bf16[128,2048]{1,0:T(8,128)(2,1)} collective-permute-done((bf16[128,2048]{1,0:T(8,128)(2,1)}, bf16[128,2048]{1,0:T(8,128)(2,1)}, u32[]{:S(2)}, u32[]{:S(2)}) %collective-permute-start.11) | collective-permute-done | bytes 524320 | tf_op jit(solution)/shard_map/ppermute | solution.py:27
  37.7 3.9 %all-to-all-start = ((bf16[4,128,512]{2,1,0:T(8,128)(2,1)}), bf16[4,128,512]{2,1,0:T(8,128)(2,1)S(1)}, u32[]{:S(2)}, u32[]{:S(2)}) async-start(bf16[4,128,512]{2,1,0:T(8,128)(2,1)} %broadcast_in_dim.142), calls=%async_computation | async-start | bytes 1048576 | tf_op jit(solution)/shard_map/all_to_all | solution.py:31
  43.7 12.2 %collective-permute-done.15 = bf16[128,2048]{1,0:T(8,128)(2,1)} collective-permute-done((bf16[128,2048]{1,0:T(8,128)(2,1)}, bf16[128,2048]{1,0:T(8,128)(2,1)}, u32[]{:S(2)}, u32[]{:S(2)}) %collective-permute-start.15) | collective-permute-done | bytes 524320 | tf_op jit(solution)/shard_map/ppermute | solution.py:27
  61.7 6.7 %two_sided.6 = bf16[128,2560]{1,0:T(8,128)(2,1)} custom-call(bf16[4,128,512]{2,1,0:T(8,128)(2,1)} %copy-done.4, bf16[4,128,512]{2,1,0:T(8,128)(2,1)} %copy-done.4, bf16[1024,2048]{1,0:T(8,128)(2,1)} %a0.7, bf16[1024,2048]{1,0:T(8,128)(2,1)} %collective-permute-done.1.a1, bf16[1024,512]{1,0:T(8,128)(2,1)} %bitcast.137, ...), custom_call_target="tpu_custom_call" | custom-call | tf_op jit(solution)/shard_map/two_sided/pallas_call | solution.py:69
  74.2 5.7 %collective-permute-done.9 = bf16[128,2048]{1,0:T(8,128)(2,1)} collective-permute-done((bf16[128,2048]{1,0:T(8,128)(2,1)}, bf16[128,2048]{1,0:T(8,128)(2,1)}, u32[]{:S(2)}, u32[]{:S(2)}) %collective-permute-start.9) | collective-permute-done | bytes 524320 | tf_op jit(solution)/shard_map/ppermute | solution.py:27
  83.2 8.0 %two_sided.11 = bf16[256,2560]{1,0:T(8,128)(2,1)} custom-call(bf16[256,2048]{1,0:T(8,128)(2,1)} %pad_maximum_fusion.2.xm.xo, bf16[256,2048]{1,0:T(8,128)(2,1)} %pad_maximum_fusion.2.xm.xo, bf16[1024,2048]{1,0:T(8,128)(2,1)} %a0.11, bf16[1024,2048]{1,0:T(8,128)(2,1)} %collective-permute-done.6.a1, bf16[1024,512]{1,0:T(8,128)(2,1)} %bitcast.132, ...), custom_call_target="tpu_custom_call" | custom-call | tf_op jit(solution)/shard_map/two_sided/pallas_call | solution.py:69
  93.6 8.1 %two_sided.10 = bf16[256,2560]{1,0:T(8,128)(2,1)} custom-call(bf16[256,2048]{1,0:T(8,128)(2,1)} %pad_maximum_fusion.1.xm.xo, bf16[256,2048]{1,0:T(8,128)(2,1)} %pad_maximum_fusion.1.xm.xo, bf16[1024,2048]{1,0:T(8,128)(2,1)} %a0.11, bf16[1024,2048]{1,0:T(8,128)(2,1)} %collective-permute-done.6.a1, bf16[1024,512]{1,0:T(8,128)(2,1)} %bitcast.133, ...), custom_call_target="tpu_custom_call" | custom-call | tf_op jit(solution)/shard_map/two_sided/pallas_call | solution.py:69
  102.1 8.0 %two_sided.9 = bf16[256,2560]{1,0:T(8,128)(2,1)} custom-call(bf16[256,2048]{1,0:T(8,128)(2,1)} %pad_maximum_fusion.xm.xo, bf16[256,2048]{1,0:T(8,128)(2,1)} %pad_maximum_fusion.xm.xo, bf16[1024,2048]{1,0:T(8,128)(2,1)} %a0.11, bf16[1024,2048]{1,0:T(8,128)(2,1)} %collective-permute-done.6.a1, bf16[1024,512]{1,0:T(8,128)(2,1)} %bitcast.134, ...), custom_call_target="tpu_custom_call" | custom-call | tf_op jit(solution)/shard_map/two_sided/pallas_call | solution.py:69
  111.3 3.6 %fusion.90 = (f32[32,2,8]{2,1,0:T(2,128)S(1)}, f32[32,2,8,256]{3,2,1,0:T(8,128)S(1)}) fusion(bf16[32,2,8,128]{3,2,1,0:T(8,128)(2,1)S(1)} %bitcast.154, bf16[32,256,2,128]{3,2,1,0:T(2,128)(2,1)} %get-tuple-element.5, pred[32,256]{1,0:T(8,128)(4,1)S(1)} %iota_compare_fusion.1), kind=kOutput, calls=%fused_computation.144 | convolution fusion | flops 33947136 | bytes 4859904 | tf_op jit(solution)/shard_map/rkgd,rckd->rkgc/dot_general | solution.py:130
  117.4 3.6 %all-to-all-start.2 = ((bf16[4,32,2048]{2,1,0:T(8,128)(2,1)}), bf16[4,32,2048]{2,1,0:T(8,128)(2,1)S(1)}, u32[]{:S(2)}, u32[]{:S(2)}) async-start(bf16[4,32,2048]{2,1,0:T(8,128)(2,1)} %broadcast_in_dim.146), calls=%async_computation.2 | async-start | bytes 1048576 | tf_op jit(solution)/shard_map/all_to_all | solution.py:31
  122.7 8.1 %two_sided.8 = bf16[256,2560]{1,0:T(8,128)(2,1)} custom-call(bf16[256,2048]{1,0:T(8,128)(2,1)} %maximum_maximum_fusion.xm.xo, bf16[256,2048]{1,0:T(8,128)(2,1)} %maximum_maximum_fusion.xm.xo, bf16[1024,2048]{1,0:T(8,128)(2,1)} %a0.11, bf16[1024,2048]{1,0:T(8,128)(2,1)} %collective-permute-done.6.a1, bf16[1024,512]{1,0:T(8,128)(2,1)} %bitcast.135, ...), custom_call_target="tpu_custom_call" | custom-call | tf_op jit(solution)/shard_map/two_sided/pallas_call | solution.py:69
  130.8 24.3 %all-to-all-done.2 = bf16[4,32,2048]{2,1,0:T(8,128)(2,1)S(1)} async-done(((bf16[4,32,2048]{2,1,0:T(8,128)(2,1)}), bf16[4,32,2048]{2,1,0:T(8,128)(2,1)S(1)}, u32[]{:S(2)}, u32[]{:S(2)}) %all-to-all-start.2) | async-done | bytes 524320 | tf_op jit(solution)/shard_map/all_to_all | solution.py:31
  155.9 5.8 %output_terms.2 = bf16[4,128,512]{2,1,0:T(8,128)(2,1)} custom-call(bf16[128,2048]{1,0:T(8,128)(2,1)} %bitcast.142, bf16[2048,1024]{1,0:T(8,128)(2,1)} %a.3, bf16[2048,1024]{1,0:T(8,128)(2,1)} %collective-permute-done.3.b), custom_call_target="tpu_custom_call" | custom-call | tf_op jit(solution)/shard_map/output_terms/pallas_call | solution.py:118
  161.7 4.7 %all-to-all-start.3 = ((bf16[4,128,512]{2,1,0:T(8,128)(2,1)}), bf16[4,128,512]{2,1,0:T(8,128)(2,1)S(1)}, u32[]{:S(2)}, u32[]{:S(2)}) async-start(bf16[4,128,512]{2,1,0:T(8,128)(2,1)} %output_terms.2), calls=%async_computation.3 | async-start | bytes 1048576 | tf_op jit(solution)/shard_map/all_to_all | solution.py:31
  169.8 4.0 %fusion.94 = (f32[16,2,8,16]{3,2,1,0:T(8,128)S(1)}, f32[16,2,8,16,16]{3,4,2,1,0:T(8,128)}) fusion(pred[16,16,16]{1,2,0:T(8,128)(4,1)S(1)} %fusion.53, bf16[16,16,2,8,128]{4,3,2,1,0:T(8,128)(2,1)S(1)} %bitcast.146, bf16[16,16,2,128]{3,2,1,0:T(2,128)(2,1)S(1)} %get-tuple-element.17), kind=kOutput, calls=%fused_computation.148 | convolution fusion | flops 17039376 | bytes 1462272 | tf_op jit(solution)/shard_map/sub | solution.py:157
  176.7 4.0 %all-to-all-done.3 = bf16[4,128,512]{2,1,0:T(8,128)(2,1)S(1)} async-done(((bf16[4,128,512]{2,1,0:T(8,128)(2,1)}), bf16[4,128,512]{2,1,0:T(8,128)(2,1)S(1)}, u32[]{:S(2)}, u32[]{:S(2)}) %all-to-all-start.3) | async-done | bytes 524320 | tf_op jit(solution)/shard_map/all_to_all | solution.py:31
  186.6 3.9 %collective-permute-start.19 = (f32[16,16]{1,0:T(8,128)S(1)}, f32[16,16]{1,0:T(8,128)S(1)}, u32[]{:S(2)}, u32[]{:S(2)}) collective-permute-start(f32[16,16]{1,0:T(8,128)S(1)} %select_reduce_fusion), channel_id=1, source_target_pairs={{0,3},{1,2},{2,1},{3,0},{4,7},{5,6},{6,5},{7,4},{8,11},{9,10},{10,... | collective-permute-start | bytes 3080 | tf_op jit(solution)/shard_map/ppermute | solution.py:27
  191.1 6.5 %collective-permute-done.19 = f32[16,16]{1,0:T(8,128)S(1)} collective-permute-done((f32[16,16]{1,0:T(8,128)S(1)}, f32[16,16]{1,0:T(8,128)S(1)}, u32[]{:S(2)}, u32[]{:S(2)}) %collective-permute-start.19) | collective-permute-done | bytes 1056 | tf_op jit(solution)/shard_map/ppermute | solution.py:27
  200.7 6.7 %two_sided.7 = bf16[128,2560]{1,0:T(8,128)(2,1)} custom-call(bf16[4,128,512]{2,1,0:T(8,128)(2,1)} %copy-done.5, bf16[4,128,512]{2,1,0:T(8,128)(2,1)} %copy-done.5, bf16[1024,2048]{1,0:T(8,128)(2,1)} %a0.7, bf16[1024,2048]{1,0:T(8,128)(2,1)} %collective-permute-done.1.a1, bf16[1024,512]{1,0:T(8,128)(2,1)} %bitcast.138, ...), custom_call_target="tpu_custom_call" | custom-call | tf_op jit(solution)/shard_map/two_sided/pallas_call | solution.py:69
  230.8 6.2 %all-to-all-done.6 = bf16[4,32,2048]{2,1,0:T(8,128)(2,1)S(1)} async-done(((bf16[4,32,2048]{2,1,0:T(8,128)(2,1)}), bf16[4,32,2048]{2,1,0:T(8,128)(2,1)S(1)}, u32[]{:S(2)}, u32[]{:S(2)}) %all-to-all-start.6) | async-done | bytes 524320 | tf_op jit(solution)/shard_map/all_to_all | solution.py:31
  237.8 5.7 %output_terms.3 = bf16[4,128,512]{2,1,0:T(8,128)(2,1)} custom-call(bf16[128,2048]{1,0:T(8,128)(2,1)} %bitcast.141, bf16[2048,1024]{1,0:T(8,128)(2,1)} %a.3, bf16[2048,1024]{1,0:T(8,128)(2,1)} %collective-permute-done.3.b), custom_call_target="tpu_custom_call" | custom-call | tf_op jit(solution)/shard_map/output_terms/pallas_call | solution.py:118
  247.1 12.8 %all-to-all-done.7 = bf16[4,128,512]{2,1,0:T(8,128)(2,1)S(1)} async-done(((bf16[4,128,512]{2,1,0:T(8,128)(2,1)}), bf16[4,128,512]{2,1,0:T(8,128)(2,1)S(1)}, u32[]{:S(2)}, u32[]{:S(2)}) %all-to-all-start.7) | async-done | bytes 524320 | tf_op jit(solution)/shard_map/all_to_all | solution.py:31
  (193 shorter events, 86.3 us)
Async XLA Ops:
  1.5 19.0 %collective-permute-start = (bf16[128,256]{1,0:T(8,128)(2,1)S(1)}, bf16[128,256]{1,0:T(8,128)(2,1)S(1)}, u32[]{:S(2)}, u32[]{:S(2)}) collective-permute-start(bf16[128,256]{1,0:T(8,128)(2,1)S(1)} %bitcast.166), channel_id=1, source_target_pairs={{0,4},{4,0},{1,5},{5,1},{2,6},{6,2},{3,7},{7,3},{8,12},{12,8},{9,1... | collective-permute-start | bytes 196616 | tf_op jit(solution)/shard_map/ppermute | solution.py:23
  2.1 54.5 %collective-permute-start.1 = (bf16[1024,2048]{1,0:T(8,128)(2,1)}, bf16[1024,2048]{1,0:T(8,128)(2,1)}, u32[]{:S(2)}, u32[]{:S(2)}) collective-permute-start(bf16[1024,2048]{1,0:T(8,128)(2,1)} %a0.7), channel_id=1, source_target_pairs={{0,4},{4,0},{1,5},{5,1},{2,6},{6,2},{3,7},{7,3},{8,12},{12,8},{9,1... | collective-permute-start | bytes 12582920 | tf_op jit(solution)/shard_map/ppermute | solution.py:23
  3.6 39.5 %collective-permute-start.2 = (bf16[1024,512]{1,0:T(8,128)(2,1)S(1)}, bf16[1024,512]{1,0:T(8,128)(2,1)}, u32[]{:S(2)}, u32[]{:S(2)}) collective-permute-start(bf16[1024,512]{1,0:T(8,128)(2,1)S(1)} %bitcast.136), channel_id=1, source_target_pairs={{0,4},{4,0},{1,5},{5,1},{2,6},{6,2},{3,7},{7,3},{8,12},{12,8},{9,1... | collective-permute-start | bytes 3145736 | tf_op jit(solution)/shard_map/ppermute | solution.py:23
  10.8 71.4 %collective-permute-start.6 = (bf16[1024,2048]{1,0:T(8,128)(2,1)}, bf16[1024,2048]{1,0:T(8,128)(2,1)}, u32[]{:S(2)}, u32[]{:S(2)}) collective-permute-start(bf16[1024,2048]{1,0:T(8,128)(2,1)} %a0.11), channel_id=1, source_target_pairs={{0,4},{4,0},{1,5},{5,1},{2,6},{6,2},{3,7},{7,3},{8,12},{12,8},{9,1... | collective-permute-start | bytes 12582920 | tf_op jit(solution)/shard_map/ppermute | solution.py:23
  23.2 18.4 %collective-permute-start.8 = (bf16[128,2048]{1,0:T(8,128)(2,1)S(1)}, bf16[128,2048]{1,0:T(8,128)(2,1)}, u32[]{:S(2)}, u32[]{:S(2)}) collective-permute-start(bf16[128,2048]{1,0:T(8,128)(2,1)S(1)} %pad_maximum_fusion.3), channel_id=1, source_target_pairs={{0,8},{8,0},{16,24},{24,16},{1,9},{9,1},{17,25},{25,17},{2,10},{10... | collective-permute-start | bytes 1572872 | tf_op jit(solution)/shard_map/ppermute | solution.py:27
  35.2 20.7 %collective-permute-start.15 = (bf16[128,2048]{1,0:T(8,128)(2,1)}, bf16[128,2048]{1,0:T(8,128)(2,1)}, u32[]{:S(2)}, u32[]{:S(2)}) collective-permute-start(bf16[128,2048]{1,0:T(8,128)(2,1)} %collective-permute-done.14), channel_id=1, source_target_pairs={{0,1},{1,0},{2,3},{3,2},{4,5},{5,4},{6,7},{7,6},{8,9},{9,8},{10,11... | collective-permute-start | bytes 1572872 | tf_op jit(solution)/shard_map/ppermute | solution.py:27
  37.7 23.2 %all-to-all-start = ((bf16[4,128,512]{2,1,0:T(8,128)(2,1)}), bf16[4,128,512]{2,1,0:T(8,128)(2,1)S(1)}, u32[]{:S(2)}, u32[]{:S(2)}) async-start(bf16[4,128,512]{2,1,0:T(8,128)(2,1)} %broadcast_in_dim.142), calls=%async_computation | async-start | bytes 1048576 | tf_op jit(solution)/shard_map/all_to_all | solution.py:31
  41.6 89.2 %collective-permute-start.3 = (bf16[2048,1024]{1,0:T(8,128)(2,1)}, bf16[2048,1024]{1,0:T(8,128)(2,1)}, u32[]{:S(2)}, u32[]{:S(2)}) collective-permute-start(bf16[2048,1024]{1,0:T(8,128)(2,1)} %a.3), channel_id=1, source_target_pairs={{0,4},{4,0},{1,5},{5,1},{2,6},{6,2},{3,7},{7,3},{8,12},{12,8},{9,1... | collective-permute-start | bytes 12582920 | tf_op jit(solution)/shard_map/ppermute | solution.py:23
  43.2 39.1 %collective-permute-start.7 = (bf16[1024,512]{1,0:T(8,128)(2,1)S(1)}, bf16[1024,512]{1,0:T(8,128)(2,1)S(1)}, u32[]{:S(2)}, u32[]{:S(2)}) collective-permute-start(bf16[1024,512]{1,0:T(8,128)(2,1)S(1)} %bitcast.131), channel_id=1, source_target_pairs={{0,4},{4,0},{1,5},{5,1},{2,6},{6,2},{3,7},{7,3},{8,12},{12,8},{9,1... | collective-permute-start | bytes 3145736 | tf_op jit(solution)/shard_map/ppermute | solution.py:23
  56.5 23.4 %collective-permute-start.9 = (bf16[128,2048]{1,0:T(8,128)(2,1)}, bf16[128,2048]{1,0:T(8,128)(2,1)}, u32[]{:S(2)}, u32[]{:S(2)}) collective-permute-start(bf16[128,2048]{1,0:T(8,128)(2,1)} %collective-permute-done.8), channel_id=1, source_target_pairs={{0,1},{1,0},{2,3},{3,2},{4,5},{5,4},{6,7},{7,6},{8,9},{9,8},{10,11... | collective-permute-start | bytes 1572872 | tf_op jit(solution)/shard_map/ppermute | solution.py:27
  68.4 42.4 %all-to-all-start.1 = ((bf16[4,32,2560]{2,1,0:T(8,128)(2,1)}), bf16[4,32,2560]{2,1,0:T(8,128)(2,1)S(1)}, u32[]{:S(2)}, u32[]{:S(2)}) async-start(bf16[4,32,2560]{2,1,0:T(8,128)(2,1)} %bitcast.140), calls=%async_computation.1 | async-start | bytes 1310720 | tf_op jit(solution)/shard_map/all_to_all | solution.py:31
  91.3 75.1 %collective-permute-start.16 = (bf16[256,2560]{1,0:T(8,128)(2,1)}, bf16[256,2560]{1,0:T(8,128)(2,1)}, u32[]{:S(2)}, u32[]{:S(2)}) collective-permute-start(bf16[256,2560]{1,0:T(8,128)(2,1)} %two_sided.11), channel_id=1, source_target_pairs={{0,24},{8,16},{16,8},{24,0},{1,25},{9,17},{17,9},{25,1},{2,26},{10... | collective-permute-start | bytes 3932168 | tf_op jit(solution)/shard_map/ppermute | solution.py:27
  101.6 64.7 %collective-permute-start.13 = (bf16[256,2560]{1,0:T(8,128)(2,1)}, bf16[256,2560]{1,0:T(8,128)(2,1)}, u32[]{:S(2)}, u32[]{:S(2)}) collective-permute-start(bf16[256,2560]{1,0:T(8,128)(2,1)} %two_sided.10), channel_id=1, source_target_pairs={{0,16},{8,24},{16,0},{24,8},{1,17},{9,25},{17,1},{25,9},{2,18},{10... | collective-permute-start | bytes 3932168 | tf_op jit(solution)/shard_map/ppermute | solution.py:27
  110.1 56.3 %collective-permute-start.10 = (bf16[256,2560]{1,0:T(8,128)(2,1)}, bf16[256,2560]{1,0:T(8,128)(2,1)}, u32[]{:S(2)}, u32[]{:S(2)}) collective-permute-start(bf16[256,2560]{1,0:T(8,128)(2,1)} %two_sided.9), channel_id=1, source_target_pairs={{0,8},{8,0},{16,24},{24,16},{1,9},{9,1},{17,25},{25,17},{2,10},{10... | collective-permute-start | bytes 3932168 | tf_op jit(solution)/shard_map/ppermute | solution.py:27
  117.4 37.7 %all-to-all-start.2 = ((bf16[4,32,2048]{2,1,0:T(8,128)(2,1)}), bf16[4,32,2048]{2,1,0:T(8,128)(2,1)S(1)}, u32[]{:S(2)}, u32[]{:S(2)}) async-start(bf16[4,32,2048]{2,1,0:T(8,128)(2,1)} %broadcast_in_dim.146), calls=%async_computation.2 | async-start | bytes 1048576 | tf_op jit(solution)/shard_map/all_to_all | solution.py:31
  161.7 19.0 %all-to-all-start.3 = ((bf16[4,128,512]{2,1,0:T(8,128)(2,1)}), bf16[4,128,512]{2,1,0:T(8,128)(2,1)S(1)}, u32[]{:S(2)}, u32[]{:S(2)}) async-start(bf16[4,128,512]{2,1,0:T(8,128)(2,1)} %output_terms.2), calls=%async_computation.3 | async-start | bytes 1048576 | tf_op jit(solution)/shard_map/all_to_all | solution.py:31
  181.6 18.2 %all-to-all-start.4 = ((bf16[4,128,512]{2,1,0:T(8,128)(2,1)}), bf16[4,128,512]{2,1,0:T(8,128)(2,1)S(1)}, u32[]{:S(2)}, u32[]{:S(2)}) async-start(bf16[4,128,512]{2,1,0:T(8,128)(2,1)} %broadcast_in_dim.148), calls=%async_computation.4 | async-start | bytes 1048576 | tf_op jit(solution)/shard_map/all_to_all | solution.py:31
  211.1 18.8 %collective-permute-start.21 = (f32[2,16]{1,0:T(2,128)S(1)}, f32[2,16]{1,0:T(2,128)S(1)}, u32[]{:S(2)}, u32[]{:S(2)}) collective-permute-start(f32[2,16]{1,0:T(2,128)S(1)} %get-tuple-element.29), channel_id=1, source_target_pairs={{0,8},{4,12},{8,0},{12,4},{16,24},{20,28},{24,16},{28,20},{1,9},{5... | collective-permute-start | bytes 392 | tf_op jit(solution)/shard_map/ppermute | solution.py:27
  213.1 17.7 %collective-permute-start.22 = (f32[2,16]{1,0:T(2,128)S(1)}, f32[2,16]{1,0:T(2,128)S(1)}, u32[]{:S(2)}, u32[]{:S(2)}) collective-permute-start(f32[2,16]{1,0:T(2,128)S(1)} %get-tuple-element.28), channel_id=1, source_target_pairs={{0,12},{4,8},{8,4},{12,0},{16,28},{20,24},{24,20},{28,16},{1,13},{... | collective-permute-start | bytes 392 | tf_op jit(solution)/shard_map/ppermute | solution.py:27
  213.1 33.9 %collective-permute-start.23 = (f32[2,16]{1,0:T(2,128)S(1)}, f32[2,16]{1,0:T(2,128)S(1)}, u32[]{:S(2)}, u32[]{:S(2)}) collective-permute-start(f32[2,16]{1,0:T(2,128)S(1)} %get-tuple-element.27), channel_id=1, source_target_pairs={{0,16},{4,20},{8,24},{12,28},{16,0},{20,4},{24,8},{28,12},{1,17},{... | collective-permute-start | bytes 392 | tf_op jit(solution)/shard_map/ppermute | solution.py:27
  214.9 32.1 %collective-permute-start.24 = (f32[2,16]{1,0:T(2,128)S(1)}, f32[2,16]{1,0:T(2,128)S(1)}, u32[]{:S(2)}, u32[]{:S(2)}) collective-permute-start(f32[2,16]{1,0:T(2,128)S(1)} %get-tuple-element.26), channel_id=1, source_target_pairs={{0,20},{4,16},{8,28},{12,24},{16,4},{20,0},{24,12},{28,8},{1,21},{... | collective-permute-start | bytes 392 | tf_op jit(solution)/shard_map/ppermute | solution.py:27
  214.9 32.2 %collective-permute-start.25 = (f32[2,16]{1,0:T(2,128)S(1)}, f32[2,16]{1,0:T(2,128)S(1)}, u32[]{:S(2)}, u32[]{:S(2)}) collective-permute-start(f32[2,16]{1,0:T(2,128)S(1)} %get-tuple-element.25), channel_id=1, source_target_pairs={{0,24},{4,28},{8,16},{12,20},{16,8},{20,12},{24,0},{28,4},{1,25},{... | collective-permute-start | bytes 392 | tf_op jit(solution)/shard_map/ppermute | solution.py:27
  229.8 17.2 %collective-permute-start.26 = (f32[2,16]{1,0:T(2,128)S(1)}, f32[2,16]{1,0:T(2,128)S(1)}, u32[]{:S(2)}, u32[]{:S(2)}) collective-permute-start(f32[2,16]{1,0:T(2,128)S(1)} %get-tuple-element.24), channel_id=1, source_target_pairs={{0,28},{4,24},{8,20},{12,16},{16,12},{20,8},{24,4},{28,0},{1,29},{... | collective-permute-start | bytes 392 | tf_op jit(solution)/shard_map/ppermute | solution.py:27
  243.5 16.3 %all-to-all-start.7 = ((bf16[4,128,512]{2,1,0:T(8,128)(2,1)}), bf16[4,128,512]{2,1,0:T(8,128)(2,1)S(1)}, u32[]{:S(2)}, u32[]{:S(2)}) async-start(bf16[4,128,512]{2,1,0:T(8,128)(2,1)} %output_terms.3), calls=%async_computation.7 | async-start | bytes 1048576 | tf_op jit(solution)/shard_map/all_to_all | solution.py:31
  (33 other events, 316.0 us)

commit v3 on v2

v3 whole, which is shorter than its diff:
```python
import jax
import jax.numpy as jnp
from jax import lax
from jax.experimental import pallas as pl
from jax.experimental.pallas import tpu as pltpu
from jax.sharding import Mesh, PartitionSpec as P

QUERY_HEADS = 64
KEY_HEADS = 8
HEAD_DIM = 128
STEPS = 2
CAPR = 2
F32 = jnp.float32
BF16 = jnp.bfloat16
SCALE = HEAD_DIM ** (-0.5)
AHEAD = 2


def dot(a, b):
    return jnp.dot(a, b, preferred_element_type=F32)


def swap(x):
    return lax.ppermute(x, "core", [(0, 1), (1, 0)])


def flip(x, axes, s, count):
    return lax.ppermute(x, axes, [(i, i ^ s) for i in range(count)])


def exchange(pieces, axes):
    return lax.all_to_all(pieces, axes, 0, 0, tiled=True)


def add_up(pieces):
    total = pieces[0].astype(F32)
    for i in range(1, pieces.shape[0]):
        total = total + pieces[i].astype(F32)
    return total


def pick(x, index, axis):
    return lax.dynamic_index_in_dim(x, index, axis, keepdims=False)


def two_sided(place, inputs, moves, moved, wide, narrow, rows, outs):
    width, n_wide = wide[0].shape
    n_narrow = narrow[0].shape[1]
    block = min(512, n_narrow)
    first = n_narrow // block
    steps = first + n_wide // block
    count = len(inputs)
    part = rows // outs

    def kernel(place, *refs):
        xs, weights, results = refs[:count], refs[count : count + 4], refs[count + 4 : count + 4 + outs]
        x, held, x_sems, w_sems = refs[count + 4 + outs :]
        j = pl.program_id(0)

        def weight_copy(i, side):
            source = weights[2 + side] if i < first else weights[side]
            at = i if i < first else i - first
            return pltpu.make_async_copy(
                source.at[:, pl.ds(at * block, block)], held.at[i, side], w_sems.at[i, side]
            )

        @pl.when(j == 0)
        def _():
            copies = [
                pltpu.make_async_copy(source, target, x_sems.at[i])
                for i, (source, target) in enumerate(moves(place, xs, x))
            ]
            for copy in copies:
                copy.start()
            for i in range(min(AHEAD, steps)):
                for side in range(2):
                    weight_copy(i, side).start()
            for copy in copies:
                copy.wait()

        for i in range(steps):

            @pl.when(j == i)
            def _(i=i):
                if i + AHEAD < steps:
                    for side in range(2):
                        weight_copy(i + AHEAD, side).start()
                weight_copy(i, 0).wait()
                weight_copy(i, 1).wait()
                total = dot(x[:, :width], held[i, 0]) + dot(x[:, width:], held[i, 1])
                for k, result in enumerate(results):
                    result[...] = total[k * part : (k + 1) * part].astype(BF16)

    return pl.pallas_call(
        kernel,
        grid_spec=pltpu.PrefetchScalarGridSpec(
            num_scalar_prefetch=1,
            grid=(steps,),
            in_specs=[pl.BlockSpec(memory_space=pl.ANY)] * (count + 4),
            out_specs=[
                pl.BlockSpec((part, block), lambda j, place: (0, jnp.where(j < first, j + n_wide // block, j - first)))
                for _ in range(outs)
            ],
            scratch_shapes=[
                pltpu.VMEM((rows, 2 * width), BF16),
                pltpu.VMEM((steps, 2, width, block), BF16),
                pltpu.SemaphoreType.DMA((moved,)),
                pltpu.SemaphoreType.DMA((steps, 2)),
            ],
        ),
        out_shape=[jax.ShapeDtypeStruct((part, n_wide + n_narrow), BF16) for _ in range(outs)],
        name="two_sided",
    )(place, *inputs, wide[0], wide[1], narrow[0], narrow[1])


def blocks_product(place, blocks, tokens, wide, narrow):
    width = wide[0].shape[0]
    part = tokens // 2
    inputs = [x for block in blocks for x in block]

    def moves(place, xs, x):
        core, odd, chip = place[0], place[1], place[2]
        refs = iter(xs)
        row = 0
        for block in blocks:
            own = [next(refs) for _ in block]
            for i in range(2):
                ref = own[i] if len(own) == 2 else own[0]
                start = 0 if len(own) == 2 else pl.multiple_of((odd ^ i) * part, part)
                base = chip * (2 * width) if ref.shape[1] > 2 * width else 0
                for side, column in enumerate((core, 1 - core)):
                    at = pl.multiple_of(base + column * width, 128)
                    yield (
                        ref.at[pl.ds(start, part), pl.ds(at, width)],
                        x.at[pl.ds(row, part), pl.ds(side * width, width)],
                    )
                row += part

    count = len(blocks)
    return two_sided(place, inputs, moves, 4 * count, wide, narrow, tokens * count, count)


def pieces_product(place, x, wide, narrow):
    zs, rows, both = x.shape
    piece = both // 2
    width = zs * piece
    if piece % 128:
        x = x.reshape(zs, rows, 2, piece).transpose(2, 1, 0, 3).reshape(2, rows, width)

    def moves(place, xs, x):
        for t in range(xs[0].shape[0]):
            for side in range(2):
                if piece % 128:
                    if t == side:
                        yield xs[0].at[t], x.at[:, pl.ds(side * width, width)]
                else:
                    source = xs[0].at[t, :, pl.ds(side * piece, piece)]
                    yield source, x.at[:, pl.ds(side * width + t * piece, piece)]

    moved = 2 if piece % 128 else 2 * zs
    return two_sided(place, [x], moves, moved, wide, narrow, rows, 1)[0]


def output_terms(x, weights, zs):
    rows, depth = x.shape
    piece = weights[0].shape[1] // zs
    if piece % 128:
        mine = dot(x, weights[0]).astype(BF16).reshape(rows, zs, piece)
        other = dot(x, weights[1]).astype(BF16).reshape(rows, zs, piece)
        return jnp.concatenate([mine, other], 2).transpose(1, 0, 2)

    def kernel(source, a, b, out, x, held, x_sem, w_sems):
        j = pl.program_id(0)

        def weight_copy(i, side):
            return pltpu.make_async_copy(
                (a, b)[side].at[:, pl.ds(i * piece, piece)], held.at[i, side], w_sems.at[i, side]
            )

        @pl.when(j == 0)
        def _():
            copy = pltpu.make_async_copy(source, x, x_sem)
            copy.start()
            for i in range(min(AHEAD, zs)):
                for side in range(2):
                    weight_copy(i, side).start()
            copy.wait()

        for i in range(zs):

            @pl.when(j == i)
            def _(i=i):
                if i + AHEAD < zs:
                    for side in range(2):
                        weight_copy(i + AHEAD, side).start()
                for side in range(2):
                    weight_copy(i, side).wait()
                    out[0, :, side * piece : (side + 1) * piece] = dot(x[...], held[i, side]).astype(BF16)

    return pl.pallas_call(
        kernel,
        grid=(zs,),
        in_specs=[pl.BlockSpec(memory_space=pl.ANY)] * 3,
        out_specs=pl.BlockSpec((1, rows, 2 * piece), lambda t: (t, 0, 0)),
        out_shape=jax.ShapeDtypeStruct((zs, rows, 2 * piece), BF16),
        scratch_shapes=[
            pltpu.VMEM((rows, depth), BF16),
            pltpu.VMEM((zs, 2, depth, piece), BF16),
            pltpu.SemaphoreType.DMA,
            pltpu.SemaphoreType.DMA((zs, 2)),
        ],
        name="output_terms",
    )(x, weights[0], weights[1])


def cached_attention(q, cache_keys, cache_values, cache_mask, new_keys, new_values, step):
    old_scores = jnp.einsum("rkgd,rckd->rkgc", q, cache_keys, preferred_element_type=F32) * SCALE
    old_scores = jnp.where(cache_mask[:, None, None, :], old_scores, -1e30)
    new_scores = jnp.einsum("rkgd,trkd->rkgt", q, new_keys, preferred_element_type=F32) * SCALE
    known = lax.broadcasted_iota(jnp.int32, new_scores.shape, 3) <= step
    new_scores = jnp.where(known, new_scores, -1e30)
    top = jnp.maximum(jnp.max(old_scores, -1), jnp.max(new_scores, -1))
    old_exp = jnp.exp(old_scores - top[..., None])
    new_exp = jnp.exp(new_scores - top[..., None])
    total = jnp.sum(old_exp, -1) + jnp.sum(new_exp, -1)
    old_weights = (old_exp / total[..., None]).astype(BF16)
    new_weights = (new_exp / total[..., None]).astype(BF16)
    mixed = jnp.einsum("rkgc,rckd->rkgd", old_weights, cache_values, preferred_element_type=F32)
    mixed = mixed + jnp.einsum("rkgt,trkd->rkgd", new_weights, new_values, preferred_element_type=F32)
    return mixed.astype(BF16)


def critic_partials(parts, last, score_weight, tok_len, heads, group):
    tokens, columns = parts[0].shape
    part = tokens // 2
    q_width = heads * group * HEAD_DIM

    def kernel(*refs):
        xs, last_ref, weight, out = refs[:-3], refs[-3], refs[-2], refs[-1]

        def total(start, size):
            at = slice(start, start + size)
            x = xs[0][:, at].astype(F32)
            for ref in xs[1:]:
                x = x + ref[:, at].astype(F32)
            return x.astype(BF16)

        row = lax.broadcasted_iota(jnp.int32, (part, part), 0)
        column = lax.broadcasted_iota(jnp.int32, (part, part), 1)
        allowed = (column >= row - row % tok_len) & (column <= last_ref[...])
        bias = jnp.where(allowed, 0.0, -1e30)
        bias = jnp.concatenate([bias] * group, 0)
        share = jnp.zeros((part, HEAD_DIM), F32)
        for head in range(heads):
            pair = total(q_width + head * 2 * HEAD_DIM, 2 * HEAD_DIM)
            start = head * group * HEAD_DIM
            wide = total(start, group * HEAD_DIM)
            queries = jnp.concatenate([wide[:, g * HEAD_DIM : (g + 1) * HEAD_DIM] for g in range(group)], 0)
            scores = SCALE * lax.dot_general(
                queries, pair[:, :HEAD_DIM], (((1,), (1,)), ((), ())), preferred_element_type=F32
            )
            scores = jnp.where(bias < 0.0, -1e30, scores)
            expo = jnp.exp(scores - jnp.max(scores, -1, keepdims=True))
            weights = (expo * (1.0 / jnp.sum(expo, -1, keepdims=True))).astype(BF16)
            mixed = dot(weights, pair[:, HEAD_DIM:]).astype(BF16).astype(F32)
            for g in range(group):
                at = slice(start + g * HEAD_DIM, start + (g + 1) * HEAD_DIM)
                share = share + mixed[g * part : (g + 1) * part] * weight[:, at].astype(F32)
        out[...] = jnp.sum(share.reshape(part // tok_len, tok_len, HEAD_DIM), -1)

    return pl.pallas_call(
        kernel,
        grid=(2,),
        in_specs=[pl.BlockSpec((part, columns), lambda i: (i, 0))] * len(parts)
        + [pl.BlockSpec((part, 1), lambda i: (i, 0)), pl.BlockSpec((1, q_width), lambda i: (0, 0))],
        out_specs=pl.BlockSpec((part // tok_len, tok_len), lambda i: (i, 0)),
        out_shape=jax.ShapeDtypeStruct((tokens // tok_len, tok_len), F32),
        name="critic_partials",
    )(*parts, last, score_weight.reshape(1, q_width))


def by_flip(x, me):
    n = x.shape[0]
    at = lax.broadcasted_iota(jnp.int32, (n, n), 0) ^ me
    chosen = at == lax.broadcasted_iota(jnp.int32, (n, n), 1)
    return jnp.sum(jnp.where(chosen.reshape((n, n) + (1,) * (x.ndim - 1)), x[None], 0.0), 1)


def per_device(
    layer_inputs,
    policy_query_weight,
    policy_key_value,
    policy_out,
    kv_cache,
    prefix_len,
    responses,
    response_len,
    assign,
    critic_query_weight,
    critic_key_value,
    score_weight,
):
    chips = lax.axis_size("chip")
    zs = lax.axis_size("tensor")
    core = lax.axis_index("core")
    chip = lax.axis_index("chip")
    odd = lax.axis_index("tensor") & 1
    shards = chips * 2
    rows = kv_cache.shape[0]
    heads = kv_cache.shape[2]
    group = QUERY_HEADS // KEY_HEADS
    width = policy_query_weight.shape[0]
    q_width = policy_query_weight.shape[1]
    piece = layer_inputs.shape[1]
    half = chips * rows
    src_rows, tok_len, model_width = responses.shape
    tokens = src_rows * tok_len
    flat = responses.reshape(tokens, model_width)

    place = jnp.stack([core, odd, chip]).astype(jnp.int32)

    def features(s, start, count):
        return lax.dynamic_slice(flat, (start, (chip ^ s) * (2 * width)), (count, 2 * width))

    def turned(x):
        return jnp.where(odd == 0, x, jnp.roll(x, src_rows // 2, 0))

    pk = policy_key_value.reshape(width, -1)
    ck = critic_key_value.reshape(width, -1)
    by_core = layer_inputs.reshape(chips, 2, rows, piece)
    kept = pick(by_core, core, 1).reshape(half, piece)
    got = swap(pick(by_core, 1 - core, 1).reshape(half, piece))
    state = jnp.concatenate([kept, got], 1)
    wq = (policy_query_weight, swap(policy_query_weight))
    wk = (pk, swap(pk))
    wo = (policy_out, swap(policy_out))
    cq = (critic_query_weight, swap(critic_query_weight))
    ck = (ck, swap(ck))

    early = [s for s in range(1, chips) if 3 * s <= 2 * (chips - 1)]
    late = [s for s in range(1, chips) if s not in early]
    leaving = {s: features(s, odd * (tokens // 2), tokens // 2) for s in range(1, chips)}
    near = {s: flip(leaving[s], "chip", s, chips) for s in leaving}
    far = {s: flip(near[s], "tensor", 1, zs) for s in near}
    cache_keys = kv_cache[..., :HEAD_DIM]
    cache_values = kv_cache[..., HEAD_DIM:]
    cache_mask = lax.broadcasted_iota(jnp.int32, (rows, kv_cache.shape[1]), 1) < prefix_len[:, None]

    def spread_out(state):
        return exchange(jnp.broadcast_to(state[None], (zs, half, 2 * piece)), "tensor")

    fresh = []

    def attend(projected, step):
        q = projected[:, :q_width].reshape(rows, heads, group, HEAD_DIM)
        fresh.append(projected[:, q_width:].reshape(rows, heads, 2 * HEAD_DIM))
        fresh_all = jnp.stack(fresh + [fresh[0]] * (STEPS - len(fresh)))
        return cached_attention(
            q,
            cache_keys,
            cache_values,
            cache_mask,
            fresh_all[..., :HEAD_DIM],
            fresh_all[..., HEAD_DIM:],
            step,
        ).reshape(rows, q_width)

    def gather_rows(attended):
        copies = jnp.broadcast_to(attended[None], (chips, rows, q_width))
        return exchange(copies, "chip").reshape(half, q_width)

    def own_features(state):
        back = swap(state[:, piece:]).reshape(chips, 1, rows, piece)
        own = state[:, :piece].reshape(chips, 1, rows, piece)
        both = jnp.where(core == 0, jnp.concatenate([own, back], 1), jnp.concatenate([back, own], 1))
        return both.reshape(shards * rows, piece)

    spread = spread_out(state)
    part = pieces_product(place, spread, wq, wk)
    arrived = exchange(part.reshape(chips, rows, -1), "chip")
    partials = {0: blocks_product(place, [[flat]], tokens, cq, ck)[0]}
    attended = attend(add_up(arrived).astype(BF16), 0)
    gathered = gather_rows(attended)
    for some in (early, late):
        blocks = [[near[s], far[s]] if s in far else [near[s]] for s in some]
        ready = blocks_product(place, blocks, tokens, cq, ck)
        for s, product in zip(some, ready):
            partials[s] = flip(product, "chip", s, chips)
    summed = add_up(exchange(output_terms(gathered, wo, zs), "tensor"))
    state = (state.astype(F32) + summed).astype(BF16)
    spread = spread_out(state)
    outputs = [own_features(state)]
    part = pieces_product(place, spread, wq, wk)
    arrived = exchange(part.reshape(chips, rows, -1), "chip")
    attended = attend(add_up(arrived).astype(BF16), 1)
    gathered = gather_rows(attended)

    lengths = turned(response_len)
    dest = assign[:, 0]
    onehot = (dest[:, None] == lax.broadcasted_iota(jnp.int32, (1, shards), 1)).astype(jnp.int32)
    rank = jnp.sum((jnp.cumsum(onehot, 0) - onehot) * onehot, 1)
    slot = turned(dest * CAPR + rank)
    chosen = lax.broadcasted_iota(jnp.int32, (shards * CAPR, src_rows), 0) == slot[None, :]
    position = lax.broadcasted_iota(jnp.int32, (src_rows, tok_len), 1)
    valid = position < lengths[:, None]
    base = lax.broadcasted_iota(jnp.int32, (src_rows, tok_len), 0) % (src_rows // 2) * tok_len
    last = (base + jnp.minimum(position, lengths[:, None] - 1)).reshape(tokens, 1)
    kept_here = chosen[:, :, None] & valid[None]
    shares = critic_partials(
        [partials[s] for s in range(chips)], last, score_weight, tok_len, heads, group
    )
    packed = jnp.sum(jnp.where(kept_here, shares[None], 0.0), 1)
    total = packed
    for s in range(1, zs):
        total = total + flip(packed, "tensor", s, zs)
    total = total.reshape(chips, 2, CAPR, tok_len)
    here = pick(total, core, 1)
    there = flip(pick(total, 1 - core, 1), "core", 1, 2)
    both = jnp.where(core == 0, jnp.stack([here, there], 1), jnp.stack([there, here], 1))
    leaving = by_flip(both, chip)
    arriving = [leaving[0]]
    for s in range(1, chips):
        arriving.append(flip(leaving[s], "chip", s, chips))
    values = by_flip(jnp.stack(arriving), chip)

    summed = add_up(exchange(output_terms(gathered, wo, zs), "tensor"))
    state = (state.astype(F32) + summed).astype(BF16)
    outputs.append(own_features(state))
    return jnp.stack(outputs), values.reshape(1, shards * CAPR, tok_len)


def solution(mesh):
    dp, tensor = mesh.shape["dp"], mesh.shape["tensor"]
    fine = Mesh(mesh.devices.reshape(dp // 2, 2, tensor), ("chip", "core", "tensor"))
    rows = ("chip", "core")
    every = ("chip", "core", "tensor")

    return jax.shard_map(
        per_device,
        mesh=fine,
        in_specs=(
            P(None, every),
            P(rows, "tensor"),
            P(rows, "tensor", None),
            P("tensor", rows),
            P(rows, None, "tensor", None),
            P(rows),
            P(rows, None, None),
            P(rows),
            P(rows, None),
            P(rows, "tensor"),
            P(rows, "tensor", None),
            P("tensor"),
        ),
        out_specs=(P(None, None, every), P(rows, None, None)),
        check_vma=False,
    )
```

time: 264 us -> 238 us (0.902)
  other arithmetic: 16.5 us -> 5.29 us
  matrix products: 17.2 us -> 9.84 us
  starting transfers between devices: 57 us -> 53 us
  local copies, waits for them, and re-layouts: 24.5 us -> 21.4 us
    all_to_all x8, waiting for transfers between devices: 49.6 us -> 26.4 us  [exchange(): return lax.all_to_all(pieces, axes, 0, 0, tiled=True)]
    ppermute x19 -> x16, waiting for transfers between devices: 38.9 us -> 56.2 us  [flip(): return lax.ppermute(x, axes, [(i, i ^ s) for i in range(count)])]
    concatenate x7 -> x0, other arithmetic: 8.93 us -> none  [the longest x3 6.96 us: per_device(): ready[s] = halves_product(jnp.concatenate([near[s], far[s]], 0), cq, ck)]
    ppermute x19 -> x16, starting transfers between devices: 25.1 us -> 17.3 us  [flip(): return lax.ppermute(x, axes, [(i, i ^ s) for i in range(count)])]
    ppermute x8, waiting for transfers between devices: 0.21 us -> 5.85 us  [swap(): return lax.ppermute(x, 'core', [(0, 1), (1, 0)])]
    sub x1 -> x0, matrix products: 3.96 us -> none  [critic_partials(): expo = jnp.exp(scores - top)]
    all_to_all x8, starting transfers between devices: 29.6 us -> 33.5 us  [exchange(): return lax.all_to_all(pieces, axes, 0, 0, tiled=True)]
    unnamed x61 -> x36, local copies, waits for them, and re-layouts: 7.71 us -> 4.26 us
  transfers between devices with their start and end apart: 35 -> 32, of which waited for: 12 -> 15; matrix products, arithmetic and copies ran while one was open for 20% -> 14% of each run, Pallas kernels for 19% -> 24%
where the time goes in v3:
time: 238 us; the launch traced here: 237 us
  waiting for transfers between devices  88.5 us (37%)
  Pallas kernels  58 us (24%)
  starting transfers between devices  53 us (22%)
  local copies, waits for them, and re-layouts  21.4 us (9%)
  matrix products  9.84 us (4%)
  other arithmetic  5.29 us (2%)
    ppermute x16, waiting for transfers between devices, flip(): return lax.ppermute(x, axes, [(i, i ^ s) for i in range(count)])  56.2 us
    pallas_call x5, Pallas kernels, two_sided(): pl.pallas_call(kernel, grid_spec=pltpu.PrefetchScalarGridSpec(num_scalar_...  40.2 us
    all_to_all x8, starting transfers between devices, exchange(): return lax.all_to_all(pieces, axes, 0, 0, tiled=True)  33.5 us
    all_to_all x8, waiting for transfers between devices, exchange(): return lax.all_to_all(pieces, axes, 0, 0, tiled=True)  26.4 us
    ppermute x16, starting transfers between devices, flip(): return lax.ppermute(x, axes, [(i, i ^ s) for i in range(count)])  17.3 us
    pallas_call x2, Pallas kernels, output_terms(): pl.pallas_call(kernel, grid=(zs,), in_specs=[pl.BlockSpec(memory_space=pl...  12.4 us
    slice x1, local copies, waits for them, and re-layouts, per_device(): cache_values = kv_cache[..., HEAD_DIM:]  8.43 us
    dot_general x2, matrix products, cached_attention(): jnp.einsum('rkgd,rckd->rkgc', q, cache_keys, preferred_element_type=F32)  7.26 us
  transfers between devices with their start and end apart: 32, of which 15 were waited for; matrix products, arithmetic and copies ran while one was open for 14% of the time, Pallas kernels for 24%

profile of v3, /device:TPU:0, one launch (start us, length us, event | category | flops | bytes accessed | tf_op | source)
XLA Modules:
  0.0 237.2 jit_solution(13734668621681635626)
XLA Ops:
  4.2 5.6 %collective-permute-done = bf16[128,256]{1,0:T(8,128)(2,1)S(1)} collective-permute-done((bf16[128,256]{1,0:T(8,128)(2,1)S(1)}, bf16[128,256]{1,0:T(8,128)(2,1)S(1)}, u32[]{:S(2)}, u32[]{:S(2)}) %collective-permute-start) | collective-permute-done | bytes 65568 | tf_op jit(solution)/shard_map/ppermute | solution.py:24
  10.7 6.2 %all-to-all-start = ((bf16[4,128,512]{2,1,0:T(8,128)(2,1)}), bf16[4,128,512]{2,1,0:T(8,128)(2,1)}, u32[]{:S(2)}, u32[]{:S(2)}) async-start(bf16[4,128,512]{2,1,0:T(8,128)(2,1)} %broadcast_in_dim.110), calls=%async_computation | async-start | bytes 1048576 | tf_op jit(solution)/shard_map/all_to_all | solution.py:32
  18.5 13.3 %all-to-all-done.refs_0_ = bf16[4,128,512]{2,1,0:T(8,128)(2,1)} async-done(((bf16[4,128,512]{2,1,0:T(8,128)(2,1)}), bf16[4,128,512]{2,1,0:T(8,128)(2,1)}, u32[]{:S(2)}, u32[]{:S(2)}) %all-to-all-start) | async-done | bytes 524320 | tf_op jit(solution)/shard_map/all_to_all | solution.py:32
  31.8 7.1 %two_sided.5 = bf16[128,2560]{1,0:T(8,128)(2,1)} custom-call(s32[3]{0:T(128)} %pad_add_fusion.place, bf16[4,128,512]{2,1,0:T(8,128)(2,1)} %all-to-all-done.refs_0_, bf16[1024,2048]{1,0:T(8,128)(2,1)} %refs_1_.4, bf16[1024,2048]{1,0:T(8,128)(2,1)} %collective-permute-done.1.refs_2_, bf16[1024,512]{1,0:T(8,128)(2,1)} %bitcast.89, ...), custom_call_target="tpu_custom_call" | custom-call | tf_op jit(solution)/shard_map/two_sided/pallas_call | solution.py:94
  38.9 3.7 %all-to-all-start.1 = ((bf16[4,32,2560]{2,1,0:T(8,128)(2,1)}), bf16[4,32,2560]{2,1,0:T(8,128)(2,1)S(1)}, u32[]{:S(2)}, u32[]{:S(2)}) async-start(bf16[4,32,2560]{2,1,0:T(8,128)(2,1)} %bitcast.94), calls=%async_computation.1 | async-start | bytes 1310720 | tf_op jit(solution)/shard_map/all_to_all | solution.py:32
  42.6 8.4 %fusion.65 = (bf16[32,256,2,128]{3,2,1,0:T(2,128)(2,1)}, bf16[32,256,2,128]{3,2,1,0:T(2,128)(2,1)}) fusion(bf16[32,256,2,256]{3,2,1,0:T(2,128)(2,1)} %param.16), kind=kLoop, calls=%fused_computation.106 | loop fusion | bytes 16777216 | tf_op jit(solution)/shard_map/slice | solution.py:346
  51.8 3.6 %fusion.72 = (f32[32,2,8]{2,1,0:T(2,128)S(1)}, f32[32,2,8,256]{3,2,1,0:T(8,128)S(1)}) fusion(bf16[32,2,8,128]{3,2,1,0:T(8,128)(2,1)S(1)} %bitcast.106, bf16[32,256,2,128]{3,2,1,0:T(2,128)(2,1)} %get-tuple-element.11, pred[32,256]{1,0:T(8,128)(4,1)S(1)} %iota_compare_fusion), kind=kOutput, calls=%fused_computation.113 | convolution fusion | flops 33947136 | bytes 4859904 | tf_op jit(solution)/shard_map/rkgd,rckd->rkgc/dot_general | solution.py:217
  57.9 4.0 %all-to-all-start.2 = ((bf16[4,32,2048]{2,1,0:T(8,128)(2,1)}), bf16[4,32,2048]{2,1,0:T(8,128)(2,1)S(1)}, u32[]{:S(2)}, u32[]{:S(2)}) async-start(bf16[4,32,2048]{2,1,0:T(8,128)(2,1)} %broadcast_in_dim.114), calls=%async_computation.2 | async-start | bytes 1048576 | tf_op jit(solution)/shard_map/all_to_all | solution.py:32
  72.1 6.2 %output_terms.2 = bf16[4,128,512]{2,1,0:T(8,128)(2,1)} custom-call(bf16[128,2048]{1,0:T(8,128)(2,1)} %bitcast.95, bf16[2048,1024]{1,0:T(8,128)(2,1)} %a.3, bf16[2048,1024]{1,0:T(8,128)(2,1)} %collective-permute-done.3.b), custom_call_target="tpu_custom_call" | custom-call | tf_op jit(solution)/shard_map/output_terms/pallas_call | solution.py:200
  84.7 7.5 %collective-permute-done.14.refs_0_ = bf16[128,2048]{1,0:T(8,128)(2,1)} collective-permute-done((bf16[128,2048]{1,0:T(8,128)(2,1)S(1)}, bf16[128,2048]{1,0:T(8,128)(2,1)}, u32[]{:S(2)}, u32[]{:S(2)}) %collective-permute-start.14) | collective-permute-done | bytes 524320 | tf_op jit(solution)/shard_map/ppermute | solution.py:28
  93.2 5.4 %all-to-all-start.4 = ((bf16[4,128,512]{2,1,0:T(8,128)(2,1)}), bf16[4,128,512]{2,1,0:T(8,128)(2,1)S(1)}, u32[]{:S(2)}, u32[]{:S(2)}) async-start(bf16[4,128,512]{2,1,0:T(8,128)(2,1)} %broadcast_in_dim.116), calls=%async_computation.4 | async-start | bytes 1048576 | tf_op jit(solution)/shard_map/all_to_all | solution.py:32
  98.6 5.7 %collective-permute-done.9.refs_1_ = bf16[128,2048]{1,0:T(8,128)(2,1)} collective-permute-done((bf16[128,2048]{1,0:T(8,128)(2,1)}, bf16[128,2048]{1,0:T(8,128)(2,1)}, u32[]{:S(2)}, u32[]{:S(2)}) %collective-permute-start.9) | collective-permute-done | bytes 524320 | tf_op jit(solution)/shard_map/ppermute | solution.py:28
  104.3 12.6 %collective-permute-done.11.refs_3_ = bf16[128,2048]{1,0:T(8,128)(2,1)} collective-permute-done((bf16[128,2048]{1,0:T(8,128)(2,1)}, bf16[128,2048]{1,0:T(8,128)(2,1)}, u32[]{:S(2)}, u32[]{:S(2)}) %collective-permute-start.11) | collective-permute-done | bytes 524320 | tf_op jit(solution)/shard_map/ppermute | solution.py:28
  116.9 10.6 %two_sided.8 = (bf16[256,2560]{1,0:T(8,128)(2,1)}, bf16[256,2560]{1,0:T(8,128)(2,1)}) custom-call(s32[3]{0:T(128)} %pad_add_fusion.place, bf16[128,2048]{1,0:T(8,128)(2,1)} %collective-permute-done.8.refs_0_, bf16[128,2048]{1,0:T(8,128)(2,1)} %collective-permute-done.9.refs_1_, bf16[128,2048]{1,0:T(8,128)(2,1)} %collective-permute-done.10.refs_2_, ...), custom_call_target="tpu_custom_call" | custom-call | tf_op jit(solution)/shard_map/two_sided/pallas_call | solution.py:94
  129.2 7.7 %two_sided.9 = bf16[256,2560]{1,0:T(8,128)(2,1)} custom-call(s32[3]{0:T(128)} %pad_add_fusion.place, bf16[128,2048]{1,0:T(8,128)(2,1)} %collective-permute-done.14.refs_0_, bf16[128,2048]{1,0:T(8,128)(2,1)} %collective-permute-done.15.refs_1_, bf16[1024,2048]{1,0:T(8,128)(2,1)} %refs_2_.1, bf16[1024,2048]{1,0:T(8,128)(2,1)} %collective-permute-done.6.refs_2_.refs_5_.refs_3_, ...), custom_call_target="tpu_custom_call" | custom-call | tf_op jit(solution)/shard_map/two_sided/pallas_call | solution.py:94
  140.0 7.1 %two_sided.6 = bf16[128,2560]{1,0:T(8,128)(2,1)} custom-call(s32[3]{0:T(128)} %pad_add_fusion.place, bf16[4,128,512]{2,1,0:T(8,128)(2,1)} %copy-done.5, bf16[1024,2048]{1,0:T(8,128)(2,1)} %refs_1_.4, bf16[1024,2048]{1,0:T(8,128)(2,1)} %collective-permute-done.1.refs_2_, bf16[1024,512]{1,0:T(8,128)(2,1)} %bitcast.90, ...), custom_call_target="tpu_custom_call" | custom-call | tf_op jit(solution)/shard_map/two_sided/pallas_call | solution.py:94
  147.1 3.7 %all-to-all-start.5 = ((bf16[4,32,2560]{2,1,0:T(8,128)(2,1)}), bf16[4,32,2560]{2,1,0:T(8,128)(2,1)S(1)}, u32[]{:S(2)}, u32[]{:S(2)}) async-start(bf16[4,32,2560]{2,1,0:T(8,128)(2,1)} %bitcast.93), calls=%async_computation.5 | async-start | bytes 1310720 | tf_op jit(solution)/shard_map/all_to_all | solution.py:32
  152.3 7.7 %two_sided.7.refs_0_ = bf16[256,2560]{1,0:T(8,128)(2,1)} custom-call(s32[3]{0:T(128)} %pad_add_fusion.place, bf16[256,8192]{1,0:T(8,128)(2,1)} %bitcast.92, bf16[1024,2048]{1,0:T(8,128)(2,1)} %refs_2_.1, bf16[1024,2048]{1,0:T(8,128)(2,1)} %collective-permute-done.6.refs_2_.refs_5_.refs_3_, bf16[1024,512]{1,0:T(8,128)(2,1)} %bitcast.87, ...), custom_call_target="tpu_custom_call" | custom-call | tf_op jit(solution)/shard_map/two_sided/pallas_call | solution.py:94
  160.0 26.8 %collective-permute-done.13.refs_2_ = bf16[256,2560]{1,0:T(8,128)(2,1)} collective-permute-done((bf16[256,2560]{1,0:T(8,128)(2,1)}, bf16[256,2560]{1,0:T(8,128)(2,1)}, u32[]{:S(2)}, u32[]{:S(2)}) %collective-permute-start.13) | collective-permute-done | bytes 1310752 | tf_op jit(solution)/shard_map/ppermute | solution.py:28
  186.8 5.3 %critic_partials.1 = f32[16,16]{1,0:T(8,128)} custom-call(bf16[256,2560]{1,0:T(8,128)(2,1)} %two_sided.7.refs_0_, bf16[256,2560]{1,0:T(8,128)(2,1)} %copy-done.8, bf16[256,2560]{1,0:T(8,128)(2,1)} %collective-permute-done.13.refs_2_, bf16[256,2560]{1,0:T(8,128)(2,1)} %collective-permute-done.16.refs_3_, s32[256,1]{1,0:T(8,128)} %add.187.refs_4_, ...), custom_call_target="tpu_custom_call" | custom-call | tf_op jit(solution)/shard_map/critic_partials/pallas_call | solution.py:271
  197.6 3.6 %fusion.74 = (f32[32,2,8]{2,1,0:T(2,128)S(1)}, f32[32,2,8,256]{3,2,1,0:T(8,128)S(1)}) fusion(bf16[32,2,8,128]{3,2,1,0:T(8,128)(2,1)S(1)} %bitcast.103, bf16[32,256,2,128]{3,2,1,0:T(2,128)(2,1)} %get-tuple-element.11, pred[32,256]{1,0:T(8,128)(4,1)S(1)} %iota_compare_fusion), kind=kOutput, calls=%fused_computation.115 | convolution fusion | flops 33947136 | bytes 4859904 | tf_op jit(solution)/shard_map/rkgd,rckd->rkgc/dot_general | solution.py:217
  207.5 6.4 %all-to-all-done.6 = bf16[4,32,2048]{2,1,0:T(8,128)(2,1)S(1)} async-done(((bf16[4,32,2048]{2,1,0:T(8,128)(2,1)}), bf16[4,32,2048]{2,1,0:T(8,128)(2,1)S(1)}, u32[]{:S(2)}, u32[]{:S(2)}) %all-to-all-start.6) | async-done | bytes 524320 | tf_op jit(solution)/shard_map/all_to_all | solution.py:32
  214.7 6.2 %output_terms.3 = bf16[4,128,512]{2,1,0:T(8,128)(2,1)} custom-call(bf16[128,2048]{1,0:T(8,128)(2,1)} %bitcast.96, bf16[2048,1024]{1,0:T(8,128)(2,1)} %a.3, bf16[2048,1024]{1,0:T(8,128)(2,1)} %collective-permute-done.3.b), custom_call_target="tpu_custom_call" | custom-call | tf_op jit(solution)/shard_map/output_terms/pallas_call | solution.py:200
  220.9 3.5 %all-to-all-start.7 = ((bf16[4,128,512]{2,1,0:T(8,128)(2,1)}), bf16[4,128,512]{2,1,0:T(8,128)(2,1)S(1)}, u32[]{:S(2)}, u32[]{:S(2)}) async-start(bf16[4,128,512]{2,1,0:T(8,128)(2,1)} %output_terms.3), calls=%async_computation.7 | async-start | bytes 1048576 | tf_op jit(solution)/shard_map/all_to_all | solution.py:32
  (153 shorter events, 57.9 us)
Async XLA Ops:
  0.6 31.2 %collective-permute-start.1 = (bf16[1024,2048]{1,0:T(8,128)(2,1)}, bf16[1024,2048]{1,0:T(8,128)(2,1)}, u32[]{:S(2)}, u32[]{:S(2)}) collective-permute-start(bf16[1024,2048]{1,0:T(8,128)(2,1)} %refs_1_.4), channel_id=1, source_target_pairs={{0,4},{4,0},{1,5},{5,1},{2,6},{6,2},{3,7},{7,3},{8,12},{12,8},{9,1... | collective-permute-start | bytes 12582920 | tf_op jit(solution)/shard_map/ppermute | solution.py:24
  2.7 29.2 %collective-permute-start.2 = (bf16[1024,512]{1,0:T(8,128)(2,1)S(1)}, bf16[1024,512]{1,0:T(8,128)(2,1)}, u32[]{:S(2)}, u32[]{:S(2)}) collective-permute-start(bf16[1024,512]{1,0:T(8,128)(2,1)S(1)} %bitcast.88), channel_id=1, source_target_pairs={{0,4},{4,0},{1,5},{5,1},{2,6},{6,2},{3,7},{7,3},{8,12},{12,8},{9,1... | collective-permute-start | bytes 3145736 | tf_op jit(solution)/shard_map/ppermute | solution.py:24
  10.7 21.1 %all-to-all-start = ((bf16[4,128,512]{2,1,0:T(8,128)(2,1)}), bf16[4,128,512]{2,1,0:T(8,128)(2,1)}, u32[]{:S(2)}, u32[]{:S(2)}) async-start(bf16[4,128,512]{2,1,0:T(8,128)(2,1)} %broadcast_in_dim.110), calls=%async_computation | async-start | bytes 1048576 | tf_op jit(solution)/shard_map/all_to_all | solution.py:32
  16.9 51.2 %collective-permute-start.3 = (bf16[2048,1024]{1,0:T(8,128)(2,1)}, bf16[2048,1024]{1,0:T(8,128)(2,1)}, u32[]{:S(2)}, u32[]{:S(2)}) collective-permute-start(bf16[2048,1024]{1,0:T(8,128)(2,1)} %a.3), channel_id=1, source_target_pairs={{0,4},{4,0},{1,5},{5,1},{2,6},{6,2},{3,7},{7,3},{8,12},{12,8},{9,1... | collective-permute-start | bytes 12582920 | tf_op jit(solution)/shard_map/ppermute | solution.py:24
  16.9 100.0 %collective-permute-start.6 = (bf16[1024,2048]{1,0:T(8,128)(2,1)}, bf16[1024,2048]{1,0:T(8,128)(2,1)}, u32[]{:S(2)}, u32[]{:S(2)}) collective-permute-start(bf16[1024,2048]{1,0:T(8,128)(2,1)} %refs_2_.1), channel_id=1, source_target_pairs={{0,4},{4,0},{1,5},{5,1},{2,6},{6,2},{3,7},{7,3},{8,12},{12,8},{9,1... | collective-permute-start | bytes 12582920 | tf_op jit(solution)/shard_map/ppermute | solution.py:24
  17.7 80.9 %collective-permute-start.7 = (bf16[1024,512]{1,0:T(8,128)(2,1)S(1)}, bf16[1024,512]{1,0:T(8,128)(2,1)S(1)}, u32[]{:S(2)}, u32[]{:S(2)}) collective-permute-start(bf16[1024,512]{1,0:T(8,128)(2,1)S(1)} %bitcast.84), channel_id=1, source_target_pairs={{0,4},{4,0},{1,5},{5,1},{2,6},{6,2},{3,7},{7,3},{8,12},{12,8},{9,1... | collective-permute-start | bytes 3145736 | tf_op jit(solution)/shard_map/ppermute | solution.py:24
  38.9 12.4 %all-to-all-start.1 = ((bf16[4,32,2560]{2,1,0:T(8,128)(2,1)}), bf16[4,32,2560]{2,1,0:T(8,128)(2,1)S(1)}, u32[]{:S(2)}, u32[]{:S(2)}) async-start(bf16[4,32,2560]{2,1,0:T(8,128)(2,1)} %bitcast.94), calls=%async_computation.1 | async-start | bytes 1310720 | tf_op jit(solution)/shard_map/all_to_all | solution.py:32
  57.9 13.4 %all-to-all-start.2 = ((bf16[4,32,2048]{2,1,0:T(8,128)(2,1)}), bf16[4,32,2048]{2,1,0:T(8,128)(2,1)S(1)}, u32[]{:S(2)}, u32[]{:S(2)}) async-start(bf16[4,32,2048]{2,1,0:T(8,128)(2,1)} %broadcast_in_dim.114), calls=%async_computation.2 | async-start | bytes 1048576 | tf_op jit(solution)/shard_map/all_to_all | solution.py:32
  64.5 18.1 %collective-permute-start.8 = (bf16[128,2048]{1,0:T(8,128)(2,1)}, bf16[128,2048]{1,0:T(8,128)(2,1)}, u32[]{:S(2)}, u32[]{:S(2)}) collective-permute-start(bf16[128,2048]{1,0:T(8,128)(2,1)} %get-tuple-element.14), channel_id=1, source_target_pairs={{0,8},{8,0},{16,24},{24,16},{1,9},{9,1},{17,25},{25,17},{2,10},{10... | collective-permute-start | bytes 1572872 | tf_op jit(solution)/shard_map/ppermute | solution.py:28
  66.5 17.6 %collective-permute-start.10 = (bf16[128,2048]{1,0:T(8,128)(2,1)}, bf16[128,2048]{1,0:T(8,128)(2,1)}, u32[]{:S(2)}, u32[]{:S(2)}) collective-permute-start(bf16[128,2048]{1,0:T(8,128)(2,1)} %get-tuple-element.13), channel_id=1, source_target_pairs={{0,16},{8,24},{16,0},{24,8},{1,17},{9,25},{17,1},{25,9},{2,18},{10... | collective-permute-start | bytes 1572872 | tf_op jit(solution)/shard_map/ppermute | solution.py:28
  68.1 24.1 %collective-permute-start.14 = (bf16[128,2048]{1,0:T(8,128)(2,1)S(1)}, bf16[128,2048]{1,0:T(8,128)(2,1)}, u32[]{:S(2)}, u32[]{:S(2)}) collective-permute-start(bf16[128,2048]{1,0:T(8,128)(2,1)S(1)} %get-tuple-element.12), channel_id=1, source_target_pairs={{0,24},{8,16},{16,8},{24,0},{1,25},{9,17},{17,9},{25,1},{2,26},{10... | collective-permute-start | bytes 1572872 | tf_op jit(solution)/shard_map/ppermute | solution.py:28
  78.4 13.9 %all-to-all-start.3 = ((bf16[4,128,512]{2,1,0:T(8,128)(2,1)}), bf16[4,128,512]{2,1,0:T(8,128)(2,1)S(1)}, u32[]{:S(2)}, u32[]{:S(2)}) async-start(bf16[4,128,512]{2,1,0:T(8,128)(2,1)} %output_terms.2), calls=%async_computation.3 | async-start | bytes 1048576 | tf_op jit(solution)/shard_map/all_to_all | solution.py:32
  82.7 21.6 %collective-permute-start.9 = (bf16[128,2048]{1,0:T(8,128)(2,1)}, bf16[128,2048]{1,0:T(8,128)(2,1)}, u32[]{:S(2)}, u32[]{:S(2)}) collective-permute-start(bf16[128,2048]{1,0:T(8,128)(2,1)} %collective-permute-done.8.refs_0_), channel_id=1, source_target_pairs={{0,1},{1,0},{2,3},{3,2},{4,5},{5,4},{6,7},{7,6},{8,9},{9,8},{10,11... | collective-permute-start | bytes 1572872 | tf_op jit(solution)/shard_map/ppermute | solution.py:28
  84.1 32.8 %collective-permute-start.11 = (bf16[128,2048]{1,0:T(8,128)(2,1)}, bf16[128,2048]{1,0:T(8,128)(2,1)}, u32[]{:S(2)}, u32[]{:S(2)}) collective-permute-start(bf16[128,2048]{1,0:T(8,128)(2,1)} %collective-permute-done.10.refs_2_), channel_id=1, source_target_pairs={{0,1},{1,0},{2,3},{3,2},{4,5},{5,4},{6,7},{7,6},{8,9},{9,8},{10,11... | collective-permute-start | bytes 1572872 | tf_op jit(solution)/shard_map/ppermute | solution.py:28
  92.2 37.0 %collective-permute-start.15 = (bf16[128,2048]{1,0:T(8,128)(2,1)}, bf16[128,2048]{1,0:T(8,128)(2,1)}, u32[]{:S(2)}, u32[]{:S(2)}) collective-permute-start(bf16[128,2048]{1,0:T(8,128)(2,1)} %collective-permute-done.14.refs_0_), channel_id=1, source_target_pairs={{0,1},{1,0},{2,3},{3,2},{4,5},{5,4},{6,7},{7,6},{8,9},{9,8},{10,11... | collective-permute-start | bytes 1572872 | tf_op jit(solution)/shard_map/ppermute | solution.py:28
  93.2 45.9 %all-to-all-start.4 = ((bf16[4,128,512]{2,1,0:T(8,128)(2,1)}), bf16[4,128,512]{2,1,0:T(8,128)(2,1)S(1)}, u32[]{:S(2)}, u32[]{:S(2)}) async-start(bf16[4,128,512]{2,1,0:T(8,128)(2,1)} %broadcast_in_dim.116), calls=%async_computation.4 | async-start | bytes 1048576 | tf_op jit(solution)/shard_map/all_to_all | solution.py:32
  127.6 32.4 %collective-permute-start.12 = (bf16[256,2560]{1,0:T(8,128)(2,1)}, bf16[256,2560]{1,0:T(8,128)(2,1)S(1)}, u32[]{:S(2)}, u32[]{:S(2)}) collective-permute-start(bf16[256,2560]{1,0:T(8,128)(2,1)} %get-tuple-element.4), channel_id=1, source_target_pairs={{0,8},{8,0},{16,24},{24,16},{1,9},{9,1},{17,25},{25,17},{2,10},{10... | collective-permute-start | bytes 3932168 | tf_op jit(solution)/shard_map/ppermute | solution.py:28
  128.3 58.5 %collective-permute-start.13 = (bf16[256,2560]{1,0:T(8,128)(2,1)}, bf16[256,2560]{1,0:T(8,128)(2,1)}, u32[]{:S(2)}, u32[]{:S(2)}) collective-permute-start(bf16[256,2560]{1,0:T(8,128)(2,1)} %get-tuple-element.5), channel_id=1, source_target_pairs={{0,16},{8,24},{16,0},{24,8},{1,17},{9,25},{17,1},{25,9},{2,18},{10... | collective-permute-start | bytes 3932168 | tf_op jit(solution)/shard_map/ppermute | solution.py:28
  136.9 49.9 %collective-permute-start.16 = (bf16[256,2560]{1,0:T(8,128)(2,1)}, bf16[256,2560]{1,0:T(8,128)(2,1)}, u32[]{:S(2)}, u32[]{:S(2)}) collective-permute-start(bf16[256,2560]{1,0:T(8,128)(2,1)} %two_sided.9), channel_id=1, source_target_pairs={{0,24},{8,16},{16,8},{24,0},{1,25},{9,17},{17,9},{25,1},{2,26},{10... | collective-permute-start | bytes 3932168 | tf_op jit(solution)/shard_map/ppermute | solution.py:28
  147.1 50.3 %all-to-all-start.5 = ((bf16[4,32,2560]{2,1,0:T(8,128)(2,1)}), bf16[4,32,2560]{2,1,0:T(8,128)(2,1)S(1)}, u32[]{:S(2)}, u32[]{:S(2)}) async-start(bf16[4,32,2560]{2,1,0:T(8,128)(2,1)} %bitcast.93), calls=%async_computation.5 | async-start | bytes 1310720 | tf_op jit(solution)/shard_map/all_to_all | solution.py:32
  192.9 14.5 %collective-permute-start.19 = (f32[16,16]{1,0:T(8,128)S(1)}, f32[16,16]{1,0:T(8,128)S(1)}, u32[]{:S(2)}, u32[]{:S(2)}) collective-permute-start(f32[16,16]{1,0:T(8,128)S(1)} %select_reduce_fusion), channel_id=1, source_target_pairs={{0,3},{1,2},{2,1},{3,0},{4,7},{5,6},{6,5},{7,4},{8,11},{9,10},{10,... | collective-permute-start | bytes 3080 | tf_op jit(solution)/shard_map/ppermute | solution.py:28
  195.1 12.4 %collective-permute-start.17 = (f32[16,16]{1,0:T(8,128)S(1)}, f32[16,16]{1,0:T(8,128)S(1)}, u32[]{:S(2)}, u32[]{:S(2)}) collective-permute-start(f32[16,16]{1,0:T(8,128)S(1)} %select_reduce_fusion), channel_id=1, source_target_pairs={{0,1},{1,0},{2,3},{3,2},{4,5},{5,4},{6,7},{7,6},{8,9},{9,8},{10,11... | collective-permute-start | bytes 3080 | tf_op jit(solution)/shard_map/ppermute | solution.py:28
  207.5 17.1 %collective-permute-start.20 = (f32[4,2,16]{2,1,0:T(2,128)S(1)}, f32[4,2,16]{2,1,0:T(2,128)S(1)}, u32[]{:S(2)}, u32[]{:S(2)}) collective-permute-start(f32[4,2,16]{2,1,0:T(2,128)S(1)} %get-tuple-element.26), channel_id=1, source_target_pairs={{0,4},{4,0},{1,5},{5,1},{2,6},{6,2},{3,7},{7,3},{8,12},{12,8},{9,1... | collective-permute-start | bytes 1544 | tf_op jit(solution)/shard_map/ppermute | solution.py:28
  220.9 13.7 %all-to-all-start.7 = ((bf16[4,128,512]{2,1,0:T(8,128)(2,1)}), bf16[4,128,512]{2,1,0:T(8,128)(2,1)S(1)}, u32[]{:S(2)}, u32[]{:S(2)}) async-start(bf16[4,128,512]{2,1,0:T(8,128)(2,1)} %output_terms.3), calls=%async_computation.7 | async-start | bytes 1048576 | tf_op jit(solution)/shard_map/all_to_all | solution.py:32
  (22 other events, 209.0 us)

commit v4 on v3

--- a/solution.py
+++ b/solution.py
@@ -43,7 +43,7 @@
     return lax.dynamic_index_in_dim(x, index, axis, keepdims=False)
 
 
-def two_sided(place, inputs, moves, moved, wide, narrow, rows, outs):
+def two_sided(place, inputs, moves, moved, wide, narrow, rows, outs, space=pl.ANY):
     width, n_wide = wide[0].shape
     n_narrow = narrow[0].shape[1]
     block = min(512, n_narrow)
@@ -96,7 +96,7 @@
         grid_spec=pltpu.PrefetchScalarGridSpec(
             num_scalar_prefetch=1,
             grid=(steps,),
-            in_specs=[pl.BlockSpec(memory_space=pl.ANY)] * (count + 4),
+            in_specs=[pl.BlockSpec(memory_space=space)] * count + [pl.BlockSpec(memory_space=pl.ANY)] * 4,
             out_specs=[
                 pl.BlockSpec((part, block), lambda j, place: (0, jnp.where(j < first, j + n_wide // block, j - first)))
                 for _ in range(outs)
@@ -158,7 +158,7 @@
                     yield source, x.at[:, pl.ds(side * width + t * piece, piece)]
 
     moved = 2 if piece % 128 else 2 * zs
-    return two_sided(place, [x], moves, moved, wide, narrow, rows, 1)[0]
+    return two_sided(place, [x], moves, moved, wide, narrow, rows, 1, pltpu.VMEM)[0]
 
 
 def output_terms(x, weights, zs):
@@ -169,7 +169,7 @@
         other = dot(x, weights[1]).astype(BF16).reshape(rows, zs, piece)
         return jnp.concatenate([mine, other], 2).transpose(1, 0, 2)
 
-    def kernel(source, a, b, out, x, held, x_sem, w_sems):
+    def kernel(x, a, b, out, held, w_sems):
         j = pl.program_id(0)
 
         def weight_copy(i, side):
@@ -179,12 +179,9 @@
 
         @pl.when(j == 0)
         def _():
-            copy = pltpu.make_async_copy(source, x, x_sem)
-            copy.start()
             for i in range(min(AHEAD, zs)):
                 for side in range(2):
                     weight_copy(i, side).start()
-            copy.wait()
 
         for i in range(zs):
 
@@ -200,13 +197,11 @@
     return pl.pallas_call(
         kernel,
         grid=(zs,),
-        in_specs=[pl.BlockSpec(memory_space=pl.ANY)] * 3,
+        in_specs=[pl.BlockSpec(memory_space=pltpu.VMEM)] + [pl.BlockSpec(memory_space=pl.ANY)] * 2,
         out_specs=pl.BlockSpec((1, rows, 2 * piece), lambda t: (t, 0, 0)),
         out_shape=jax.ShapeDtypeStruct((zs, rows, 2 * piece), BF16),
         scratch_shapes=[
-            pltpu.VMEM((rows, depth), BF16),
             pltpu.VMEM((zs, 2, depth, piece), BF16),
-            pltpu.SemaphoreType.DMA,
             pltpu.SemaphoreType.DMA((zs, 2)),
         ],
         name="output_terms",
@@ -337,11 +332,13 @@
     cq = (critic_query_weight, swap(critic_query_weight))
     ck = (ck, swap(ck))
 
-    early = [s for s in range(1, chips) if 3 * s <= 2 * (chips - 1)]
-    late = [s for s in range(1, chips) if s not in early]
-    leaving = {s: features(s, odd * (tokens // 2), tokens // 2) for s in range(1, chips)}
-    near = {s: flip(leaving[s], "chip", s, chips) for s in leaving}
-    far = {s: flip(near[s], "tensor", 1, zs) for s in near}
+    early = [s for s in range(2, chips) if 3 * s <= 2 * (chips - 1)]
+    late = [s for s in range(2, chips) if s not in early]
+    near = {1: flip(features(1, 0, tokens), "chip", 1, chips)}
+    for s in early + late:
+        leaving = features(s, odd * (tokens // 2), tokens // 2)
+        near[s] = flip(leaving, "chip", s, chips)
+    far = {s: flip(near[s], "tensor", 1, zs) for s in early + late}
     cache_keys = kv_cache[..., :HEAD_DIM]
     cache_values = kv_cache[..., HEAD_DIM:]
     cache_mask = lax.broadcasted_iota(jnp.int32, (rows, kv_cache.shape[1]), 1) < prefix_len[:, None]
@@ -381,7 +378,7 @@
     partials = {0: blocks_product(place, [[flat]], tokens, cq, ck)[0]}
     attended = attend(add_up(arrived).astype(BF16), 0)
     gathered = gather_rows(attended)
-    for some in (early, late):
+    for some in ([1], early, late):
         blocks = [[near[s], far[s]] if s in far else [near[s]] for s in some]
         ready = blocks_product(place, blocks, tokens, cq, ck)
         for s, product in zip(some, ready):

time: 238 us -> 241 us (1.013)
  waiting for transfers between devices: 88.5 us -> 82.4 us
  Pallas kernels: 58 us -> 64 us
  local copies, waits for them, and re-layouts: 21.4 us -> 24.2 us
    pallas_call x5 -> x6, Pallas kernels: 40.2 us -> 45.9 us  [two_sided(): pl.pallas_call(kernel, grid_spec=pltpu.PrefetchScalarGridSpec(num_scalar_...]
    ppermute x16 -> x15, waiting for transfers between devices: 56.2 us -> 51.8 us  [flip(): return lax.ppermute(x, axes, [(i, i ^ s) for i in range(count)])]
    ppermute x16 -> x15, starting transfers between devices: 17.3 us -> 17.3 us  [flip(): return lax.ppermute(x, axes, [(i, i ^ s) for i in range(count)])]
  transfers between devices with their start and end apart: 32 -> 31, of which waited for: 15 -> 12; matrix products, arithmetic and copies ran while one was open for 14% -> 15% of each run, Pallas kernels for 24% -> 27%
where the time goes in v4:
time: 241 us; the launch traced here: 239 us
  waiting for transfers between devices  82.4 us (34%)
  Pallas kernels  64 us (27%)
  starting transfers between devices  52.4 us (22%)
  local copies, waits for them, and re-layouts  24.2 us (10%)
  matrix products  9.84 us (4%)
  other arithmetic  5.31 us (2%)
    ppermute x15, waiting for transfers between devices, flip(): return lax.ppermute(x, axes, [(i, i ^ s) for i in range(count)])  51.8 us
    pallas_call x6, Pallas kernels, two_sided(): pl.pallas_call(kernel, grid_spec=pltpu.PrefetchScalarGridSpec(num_scalar_...  45.9 us
    all_to_all x8, starting transfers between devices, exchange(): return lax.all_to_all(pieces, axes, 0, 0, tiled=True)  32.9 us
    all_to_all x8, waiting for transfers between devices, exchange(): return lax.all_to_all(pieces, axes, 0, 0, tiled=True)  24.8 us
    ppermute x15, starting transfers between devices, flip(): return lax.ppermute(x, axes, [(i, i ^ s) for i in range(count)])  17.3 us
    pallas_call x2, Pallas kernels, output_terms(): pl.pallas_call(kernel, grid=(zs,), in_specs=[pl.BlockSpec(memory_space=pl...  12.9 us
    slice x1, local copies, waits for them, and re-layouts, per_device(): cache_values = kv_cache[..., HEAD_DIM:]  8.43 us
    dot_general x2, matrix products, cached_attention(): jnp.einsum('rkgd,rckd->rkgc', q, cache_keys, preferred_element_type=F32)  7.26 us
  transfers between devices with their start and end apart: 31, of which 12 were waited for; matrix products, arithmetic and copies ran while one was open for 15% of the time, Pallas kernels for 27%

profile of v4, /device:TPU:0, one launch (start us, length us, event | category | flops | bytes accessed | tf_op | source)
XLA Modules:
  0.0 239.4 jit_solution(11892921198034151656)
XLA Ops:
  4.2 5.6 %collective-permute-done = bf16[128,256]{1,0:T(8,128)(2,1)S(1)} collective-permute-done((bf16[128,256]{1,0:T(8,128)(2,1)S(1)}, bf16[128,256]{1,0:T(8,128)(2,1)S(1)}, u32[]{:S(2)}, u32[]{:S(2)}) %collective-permute-start) | collective-permute-done | bytes 65568 | tf_op jit(solution)/shard_map/ppermute | solution.py:24
  10.7 6.2 %all-to-all-start = ((bf16[4,128,512]{2,1,0:T(8,128)(2,1)}), bf16[4,128,512]{2,1,0:T(8,128)(2,1)}, u32[]{:S(2)}, u32[]{:S(2)}) async-start(bf16[4,128,512]{2,1,0:T(8,128)(2,1)} %broadcast_in_dim.110), calls=%async_computation | async-start | bytes 1048576 | tf_op jit(solution)/shard_map/all_to_all | solution.py:32
  18.6 13.3 %all-to-all-done.refs_0_ = bf16[4,128,512]{2,1,0:T(8,128)(2,1)} async-done(((bf16[4,128,512]{2,1,0:T(8,128)(2,1)}), bf16[4,128,512]{2,1,0:T(8,128)(2,1)}, u32[]{:S(2)}, u32[]{:S(2)}) %all-to-all-start) | async-done | bytes 524320 | tf_op jit(solution)/shard_map/all_to_all | solution.py:32
  31.8 7.6 %two_sided.6 = bf16[128,2560]{1,0:T(8,128)(2,1)} custom-call(s32[3]{0:T(128)} %pad_add_fusion.place, bf16[4,128,512]{2,1,0:T(8,128)(2,1)} %all-to-all-done.refs_0_, bf16[1024,2048]{1,0:T(8,128)(2,1)} %refs_1_.5, bf16[1024,2048]{1,0:T(8,128)(2,1)} %collective-permute-done.1.refs_2_, bf16[1024,512]{1,0:T(8,128)(2,1)} %bitcast.93, ...), custom_call_target="tpu_custom_call" | custom-call | tf_op jit(solution)/shard_map/two_sided/pallas_call | solution.py:94
  39.4 3.7 %all-to-all-start.1 = ((bf16[4,32,2560]{2,1,0:T(8,128)(2,1)}), bf16[4,32,2560]{2,1,0:T(8,128)(2,1)S(1)}, u32[]{:S(2)}, u32[]{:S(2)}) async-start(bf16[4,32,2560]{2,1,0:T(8,128)(2,1)} %bitcast.96), calls=%async_computation.1 | async-start | bytes 1310720 | tf_op jit(solution)/shard_map/all_to_all | solution.py:32
  43.1 8.4 %fusion.65 = (bf16[32,256,2,128]{3,2,1,0:T(2,128)(2,1)}, bf16[32,256,2,128]{3,2,1,0:T(2,128)(2,1)}) fusion(bf16[32,256,2,256]{3,2,1,0:T(2,128)(2,1)} %param.16), kind=kLoop, calls=%fused_computation.107 | loop fusion | bytes 16777216 | tf_op jit(solution)/shard_map/slice | solution.py:343
  52.3 3.6 %fusion.72 = (f32[32,2,8]{2,1,0:T(2,128)S(1)}, f32[32,2,8,256]{3,2,1,0:T(8,128)S(1)}) fusion(bf16[32,2,8,128]{3,2,1,0:T(8,128)(2,1)S(1)} %bitcast.108, bf16[32,256,2,128]{3,2,1,0:T(2,128)(2,1)} %get-tuple-element.7, pred[32,256]{1,0:T(8,128)(4,1)S(1)} %iota_compare_fusion), kind=kOutput, calls=%fused_computation.114 | convolution fusion | flops 33947136 | bytes 4859904 | tf_op jit(solution)/shard_map/rkgd,rckd->rkgc/dot_general | solution.py:212
  58.4 4.0 %all-to-all-start.2 = ((bf16[4,32,2048]{2,1,0:T(8,128)(2,1)}), bf16[4,32,2048]{2,1,0:T(8,128)(2,1)S(1)}, u32[]{:S(2)}, u32[]{:S(2)}) async-start(bf16[4,32,2048]{2,1,0:T(8,128)(2,1)} %broadcast_in_dim.114), calls=%async_computation.2 | async-start | bytes 1048576 | tf_op jit(solution)/shard_map/all_to_all | solution.py:32
  72.5 6.5 %output_terms.2 = bf16[4,128,512]{2,1,0:T(8,128)(2,1)} custom-call(bf16[128,2048]{1,0:T(8,128)(2,1)} %bitcast.97, bf16[2048,1024]{1,0:T(8,128)(2,1)} %a.3, bf16[2048,1024]{1,0:T(8,128)(2,1)} %collective-permute-done.3.b), custom_call_target="tpu_custom_call" | custom-call | tf_op jit(solution)/shard_map/output_terms/pallas_call | solution.py:197
  79.0 3.5 %all-to-all-start.3 = ((bf16[4,128,512]{2,1,0:T(8,128)(2,1)}), bf16[4,128,512]{2,1,0:T(8,128)(2,1)S(1)}, u32[]{:S(2)}, u32[]{:S(2)}) async-start(bf16[4,128,512]{2,1,0:T(8,128)(2,1)} %output_terms.2), calls=%async_computation.3 | async-start | bytes 1048576 | tf_op jit(solution)/shard_map/all_to_all | solution.py:32
  84.9 18.9 %collective-permute-done.13.refs_0_ = bf16[128,2048]{1,0:T(8,128)(2,1)} collective-permute-done((bf16[128,2048]{1,0:T(8,128)(2,1)S(1)}, bf16[128,2048]{1,0:T(8,128)(2,1)}, u32[]{:S(2)}, u32[]{:S(2)}) %collective-permute-start.13) | collective-permute-done | bytes 524320 | tf_op jit(solution)/shard_map/ppermute | solution.py:28
  104.9 3.6 %all-to-all-start.4 = ((bf16[4,128,512]{2,1,0:T(8,128)(2,1)}), bf16[4,128,512]{2,1,0:T(8,128)(2,1)S(1)}, u32[]{:S(2)}, u32[]{:S(2)}) async-start(bf16[4,128,512]{2,1,0:T(8,128)(2,1)} %broadcast_in_dim.116), calls=%async_computation.4 | async-start | bytes 1048576 | tf_op jit(solution)/shard_map/all_to_all | solution.py:32
  109.5 7.7 %two_sided.9 = bf16[256,2560]{1,0:T(8,128)(2,1)} custom-call(s32[3]{0:T(128)} %pad_add_fusion.place, bf16[256,2048]{1,0:T(8,128)(2,1)} %collective-permute-done.8.refs_0_, bf16[1024,2048]{1,0:T(8,128)(2,1)} %refs_2_.3, bf16[1024,2048]{1,0:T(8,128)(2,1)} %collective-permute-done.6.refs_2_.refs_3_, bf16[1024,512]{1,0:T(8,128)(2,1)} %bitcast.85, ...), custom_call_target="tpu_custom_call" | custom-call | tf_op jit(solution)/shard_map/two_sided/pallas_call | solution.py:94
  117.8 7.7 %two_sided.10 = bf16[256,2560]{1,0:T(8,128)(2,1)} custom-call(s32[3]{0:T(128)} %pad_add_fusion.place, bf16[128,2048]{1,0:T(8,128)(2,1)} %collective-permute-done.10.refs_0_, bf16[128,2048]{1,0:T(8,128)(2,1)} %collective-permute-done.11.refs_1_, bf16[1024,2048]{1,0:T(8,128)(2,1)} %refs_2_.3, bf16[1024,2048]{1,0:T(8,128)(2,1)} %collective-permute-done.6.refs_2_.refs_3_, ...), custom_call_target="tpu_custom_call" | custom-call | tf_op jit(solution)/shard_map/two_sided/pallas_call | solution.py:94
  125.8 7.7 %two_sided.11 = bf16[256,2560]{1,0:T(8,128)(2,1)} custom-call(s32[3]{0:T(128)} %pad_add_fusion.place, bf16[128,2048]{1,0:T(8,128)(2,1)} %collective-permute-done.13.refs_0_, bf16[128,2048]{1,0:T(8,128)(2,1)} %collective-permute-done.14.refs_1_, bf16[1024,2048]{1,0:T(8,128)(2,1)} %refs_2_.3, bf16[1024,2048]{1,0:T(8,128)(2,1)} %collective-permute-done.6.refs_2_.refs_3_, ...), custom_call_target="tpu_custom_call" | custom-call | tf_op jit(solution)/shard_map/two_sided/pallas_call | solution.py:94
  137.3 7.6 %two_sided.7 = bf16[128,2560]{1,0:T(8,128)(2,1)} custom-call(s32[3]{0:T(128)} %pad_add_fusion.place, bf16[4,128,512]{2,1,0:T(8,128)(2,1)} %copy-done.5, bf16[1024,2048]{1,0:T(8,128)(2,1)} %refs_1_.5, bf16[1024,2048]{1,0:T(8,128)(2,1)} %collective-permute-done.1.refs_2_, bf16[1024,512]{1,0:T(8,128)(2,1)} %bitcast.94, ...), custom_call_target="tpu_custom_call" | custom-call | tf_op jit(solution)/shard_map/two_sided/pallas_call | solution.py:94
  144.9 3.7 %all-to-all-start.5 = ((bf16[4,32,2560]{2,1,0:T(8,128)(2,1)}), bf16[4,32,2560]{2,1,0:T(8,128)(2,1)S(1)}, u32[]{:S(2)}, u32[]{:S(2)}) async-start(bf16[4,32,2560]{2,1,0:T(8,128)(2,1)} %bitcast.95), calls=%async_computation.5 | async-start | bytes 1310720 | tf_op jit(solution)/shard_map/all_to_all | solution.py:32
  150.1 7.7 %two_sided.8.refs_0_ = bf16[256,2560]{1,0:T(8,128)(2,1)} custom-call(s32[3]{0:T(128)} %pad_add_fusion.place, bf16[256,8192]{1,0:T(8,128)(2,1)} %bitcast.91, bf16[1024,2048]{1,0:T(8,128)(2,1)} %refs_2_.3, bf16[1024,2048]{1,0:T(8,128)(2,1)} %collective-permute-done.6.refs_2_.refs_3_, bf16[1024,512]{1,0:T(8,128)(2,1)} %bitcast.88, bf16[1024,512]{1,0:T(8,128)(2,1)} %copy-done.1), custom_call_target="tpu_custom_call" | custom-call | tf_op jit(solution)/shard_map/two_sided/pallas_call | solution.py:94
  157.8 29.8 %collective-permute-done.12.refs_2_ = bf16[256,2560]{1,0:T(8,128)(2,1)} collective-permute-done((bf16[256,2560]{1,0:T(8,128)(2,1)}, bf16[256,2560]{1,0:T(8,128)(2,1)}, u32[]{:S(2)}, u32[]{:S(2)}) %collective-permute-start.12) | collective-permute-done | bytes 1310752 | tf_op jit(solution)/shard_map/ppermute | solution.py:28
  187.6 5.2 %critic_partials.1 = f32[16,16]{1,0:T(8,128)} custom-call(bf16[256,2560]{1,0:T(8,128)(2,1)} %two_sided.8.refs_0_, bf16[256,2560]{1,0:T(8,128)(2,1)} %copy-done.8, bf16[256,2560]{1,0:T(8,128)(2,1)} %collective-permute-done.12.refs_2_, bf16[256,2560]{1,0:T(8,128)(2,1)} %collective-permute-done.15.refs_3_, s32[256,1]{1,0:T(8,128)} %add.186.refs_4_, ...), custom_call_target="tpu_custom_call" | custom-call | tf_op jit(solution)/shard_map/critic_partials/pallas_call | solution.py:266
  198.3 3.6 %fusion.74 = (f32[32,2,8]{2,1,0:T(2,128)S(1)}, f32[32,2,8,256]{3,2,1,0:T(8,128)S(1)}) fusion(bf16[32,2,8,128]{3,2,1,0:T(8,128)(2,1)S(1)} %bitcast.105, bf16[32,256,2,128]{3,2,1,0:T(2,128)(2,1)} %get-tuple-element.7, pred[32,256]{1,0:T(8,128)(4,1)S(1)} %iota_compare_fusion), kind=kOutput, calls=%fused_computation.116 | convolution fusion | flops 33947136 | bytes 4859904 | tf_op jit(solution)/shard_map/rkgd,rckd->rkgc/dot_general | solution.py:212
  208.3 6.4 %all-to-all-done.6 = bf16[4,32,2048]{2,1,0:T(8,128)(2,1)S(1)} async-done(((bf16[4,32,2048]{2,1,0:T(8,128)(2,1)}), bf16[4,32,2048]{2,1,0:T(8,128)(2,1)S(1)}, u32[]{:S(2)}, u32[]{:S(2)}) %all-to-all-start.6) | async-done | bytes 524320 | tf_op jit(solution)/shard_map/all_to_all | solution.py:32
  215.5 6.5 %output_terms.3 = bf16[4,128,512]{2,1,0:T(8,128)(2,1)} custom-call(bf16[128,2048]{1,0:T(8,128)(2,1)} %bitcast.98, bf16[2048,1024]{1,0:T(8,128)(2,1)} %a.3, bf16[2048,1024]{1,0:T(8,128)(2,1)} %collective-permute-done.3.b), custom_call_target="tpu_custom_call" | custom-call | tf_op jit(solution)/shard_map/output_terms/pallas_call | solution.py:197
  222.0 4.6 %all-to-all-start.7 = ((bf16[4,128,512]{2,1,0:T(8,128)(2,1)}), bf16[4,128,512]{2,1,0:T(8,128)(2,1)S(1)}, u32[]{:S(2)}, u32[]{:S(2)}) async-start(bf16[4,128,512]{2,1,0:T(8,128)(2,1)} %output_terms.3), calls=%async_computation.7 | async-start | bytes 1048576 | tf_op jit(solution)/shard_map/all_to_all | solution.py:32
  (153 shorter events, 55.0 us)
Async XLA Ops:
  0.6 31.2 %collective-permute-start.1 = (bf16[1024,2048]{1,0:T(8,128)(2,1)}, bf16[1024,2048]{1,0:T(8,128)(2,1)}, u32[]{:S(2)}, u32[]{:S(2)}) collective-permute-start(bf16[1024,2048]{1,0:T(8,128)(2,1)} %refs_1_.5), channel_id=1, source_target_pairs={{0,4},{4,0},{1,5},{5,1},{2,6},{6,2},{3,7},{7,3},{8,12},{12,8},{9,1... | collective-permute-start | bytes 12582920 | tf_op jit(solution)/shard_map/ppermute | solution.py:24
  2.7 29.2 %collective-permute-start.2 = (bf16[1024,512]{1,0:T(8,128)(2,1)S(1)}, bf16[1024,512]{1,0:T(8,128)(2,1)}, u32[]{:S(2)}, u32[]{:S(2)}) collective-permute-start(bf16[1024,512]{1,0:T(8,128)(2,1)S(1)} %bitcast.92), channel_id=1, source_target_pairs={{0,4},{4,0},{1,5},{5,1},{2,6},{6,2},{3,7},{7,3},{8,12},{12,8},{9,1... | collective-permute-start | bytes 3145736 | tf_op jit(solution)/shard_map/ppermute | solution.py:24
  10.7 21.1 %all-to-all-start = ((bf16[4,128,512]{2,1,0:T(8,128)(2,1)}), bf16[4,128,512]{2,1,0:T(8,128)(2,1)}, u32[]{:S(2)}, u32[]{:S(2)}) async-start(bf16[4,128,512]{2,1,0:T(8,128)(2,1)} %broadcast_in_dim.110), calls=%async_computation | async-start | bytes 1048576 | tf_op jit(solution)/shard_map/all_to_all | solution.py:32
  16.9 53.4 %collective-permute-start.3 = (bf16[2048,1024]{1,0:T(8,128)(2,1)}, bf16[2048,1024]{1,0:T(8,128)(2,1)}, u32[]{:S(2)}, u32[]{:S(2)}) collective-permute-start(bf16[2048,1024]{1,0:T(8,128)(2,1)} %a.3), channel_id=1, source_target_pairs={{0,4},{4,0},{1,5},{5,1},{2,6},{6,2},{3,7},{7,3},{8,12},{12,8},{9,1... | collective-permute-start | bytes 12582920 | tf_op jit(solution)/shard_map/ppermute | solution.py:24
  16.9 91.6 %collective-permute-start.6 = (bf16[1024,2048]{1,0:T(8,128)(2,1)}, bf16[1024,2048]{1,0:T(8,128)(2,1)}, u32[]{:S(2)}, u32[]{:S(2)}) collective-permute-start(bf16[1024,2048]{1,0:T(8,128)(2,1)} %refs_2_.3), channel_id=1, source_target_pairs={{0,4},{4,0},{1,5},{5,1},{2,6},{6,2},{3,7},{7,3},{8,12},{12,8},{9,1... | collective-permute-start | bytes 12582920 | tf_op jit(solution)/shard_map/ppermute | solution.py:24
  17.7 90.9 %collective-permute-start.7 = (bf16[1024,512]{1,0:T(8,128)(2,1)S(1)}, bf16[1024,512]{1,0:T(8,128)(2,1)S(1)}, u32[]{:S(2)}, u32[]{:S(2)}) collective-permute-start(bf16[1024,512]{1,0:T(8,128)(2,1)S(1)} %bitcast.84), channel_id=1, source_target_pairs={{0,4},{4,0},{1,5},{5,1},{2,6},{6,2},{3,7},{7,3},{8,12},{12,8},{9,1... | collective-permute-start | bytes 3145736 | tf_op jit(solution)/shard_map/ppermute | solution.py:24
  39.4 12.5 %all-to-all-start.1 = ((bf16[4,32,2560]{2,1,0:T(8,128)(2,1)}), bf16[4,32,2560]{2,1,0:T(8,128)(2,1)S(1)}, u32[]{:S(2)}, u32[]{:S(2)}) async-start(bf16[4,32,2560]{2,1,0:T(8,128)(2,1)} %bitcast.96), calls=%async_computation.1 | async-start | bytes 1310720 | tf_op jit(solution)/shard_map/all_to_all | solution.py:32
  58.4 13.4 %all-to-all-start.2 = ((bf16[4,32,2048]{2,1,0:T(8,128)(2,1)}), bf16[4,32,2048]{2,1,0:T(8,128)(2,1)S(1)}, u32[]{:S(2)}, u32[]{:S(2)}) async-start(bf16[4,32,2048]{2,1,0:T(8,128)(2,1)} %broadcast_in_dim.114), calls=%async_computation.2 | async-start | bytes 1048576 | tf_op jit(solution)/shard_map/all_to_all | solution.py:32
  64.7 43.8 %collective-permute-start.8 = (bf16[256,2048]{1,0:T(8,128)(2,1)}, bf16[256,2048]{1,0:T(8,128)(2,1)}, u32[]{:S(2)}, u32[]{:S(2)}) collective-permute-start(bf16[256,2048]{1,0:T(8,128)(2,1)} %constant_dynamic-slice_fusion.1), channel_id=1, source_target_pairs={{0,8},{8,0},{16,24},{24,16},{1,9},{9,1},{17,25},{25,17},{2,10},{10... | collective-permute-start | bytes 3145736 | tf_op jit(solution)/shard_map/ppermute | solution.py:28
  68.8 14.1 %collective-permute-start.10 = (bf16[128,2048]{1,0:T(8,128)(2,1)}, bf16[128,2048]{1,0:T(8,128)(2,1)}, u32[]{:S(2)}, u32[]{:S(2)}) collective-permute-start(bf16[128,2048]{1,0:T(8,128)(2,1)} %get-tuple-element.9), channel_id=1, source_target_pairs={{0,16},{8,24},{16,0},{24,8},{1,17},{9,25},{17,1},{25,9},{2,18},{10... | collective-permute-start | bytes 1572872 | tf_op jit(solution)/shard_map/ppermute | solution.py:28
  70.3 33.5 %collective-permute-start.13 = (bf16[128,2048]{1,0:T(8,128)(2,1)S(1)}, bf16[128,2048]{1,0:T(8,128)(2,1)}, u32[]{:S(2)}, u32[]{:S(2)}) collective-permute-start(bf16[128,2048]{1,0:T(8,128)(2,1)S(1)} %get-tuple-element.8), channel_id=1, source_target_pairs={{0,24},{8,16},{16,8},{24,0},{1,25},{9,17},{17,9},{25,1},{2,26},{10... | collective-permute-start | bytes 1572872 | tf_op jit(solution)/shard_map/ppermute | solution.py:28
  79.0 24.9 %all-to-all-start.3 = ((bf16[4,128,512]{2,1,0:T(8,128)(2,1)}), bf16[4,128,512]{2,1,0:T(8,128)(2,1)S(1)}, u32[]{:S(2)}, u32[]{:S(2)}) async-start(bf16[4,128,512]{2,1,0:T(8,128)(2,1)} %output_terms.2), calls=%async_computation.3 | async-start | bytes 1048576 | tf_op jit(solution)/shard_map/all_to_all | solution.py:32
  82.9 34.9 %collective-permute-start.11 = (bf16[128,2048]{1,0:T(8,128)(2,1)}, bf16[128,2048]{1,0:T(8,128)(2,1)}, u32[]{:S(2)}, u32[]{:S(2)}) collective-permute-start(bf16[128,2048]{1,0:T(8,128)(2,1)} %collective-permute-done.10.refs_0_), channel_id=1, source_target_pairs={{0,1},{1,0},{2,3},{3,2},{4,5},{5,4},{6,7},{7,6},{8,9},{9,8},{10,11... | collective-permute-start | bytes 1572872 | tf_op jit(solution)/shard_map/ppermute | solution.py:28
  103.8 22.0 %collective-permute-start.14 = (bf16[128,2048]{1,0:T(8,128)(2,1)}, bf16[128,2048]{1,0:T(8,128)(2,1)}, u32[]{:S(2)}, u32[]{:S(2)}) collective-permute-start(bf16[128,2048]{1,0:T(8,128)(2,1)} %collective-permute-done.13.refs_0_), channel_id=1, source_target_pairs={{0,1},{1,0},{2,3},{3,2},{4,5},{5,4},{6,7},{7,6},{8,9},{9,8},{10,11... | collective-permute-start | bytes 1572872 | tf_op jit(solution)/shard_map/ppermute | solution.py:28
  104.9 31.6 %all-to-all-start.4 = ((bf16[4,128,512]{2,1,0:T(8,128)(2,1)}), bf16[4,128,512]{2,1,0:T(8,128)(2,1)S(1)}, u32[]{:S(2)}, u32[]{:S(2)}) async-start(bf16[4,128,512]{2,1,0:T(8,128)(2,1)} %broadcast_in_dim.116), calls=%async_computation.4 | async-start | bytes 1048576 | tf_op jit(solution)/shard_map/all_to_all | solution.py:32
  117.2 40.6 %collective-permute-start.9 = (bf16[256,2560]{1,0:T(8,128)(2,1)}, bf16[256,2560]{1,0:T(8,128)(2,1)S(1)}, u32[]{:S(2)}, u32[]{:S(2)}) collective-permute-start(bf16[256,2560]{1,0:T(8,128)(2,1)} %two_sided.9), channel_id=1, source_target_pairs={{0,8},{8,0},{16,24},{24,16},{1,9},{9,1},{17,25},{25,17},{2,10},{10... | collective-permute-start | bytes 3932168 | tf_op jit(solution)/shard_map/ppermute | solution.py:28
  125.5 62.2 %collective-permute-start.12 = (bf16[256,2560]{1,0:T(8,128)(2,1)}, bf16[256,2560]{1,0:T(8,128)(2,1)}, u32[]{:S(2)}, u32[]{:S(2)}) collective-permute-start(bf16[256,2560]{1,0:T(8,128)(2,1)} %two_sided.10), channel_id=1, source_target_pairs={{0,16},{8,24},{16,0},{24,8},{1,17},{9,25},{17,1},{25,9},{2,18},{10... | collective-permute-start | bytes 3932168 | tf_op jit(solution)/shard_map/ppermute | solution.py:28
  133.5 54.1 %collective-permute-start.15 = (bf16[256,2560]{1,0:T(8,128)(2,1)}, bf16[256,2560]{1,0:T(8,128)(2,1)}, u32[]{:S(2)}, u32[]{:S(2)}) collective-permute-start(bf16[256,2560]{1,0:T(8,128)(2,1)} %two_sided.11), channel_id=1, source_target_pairs={{0,24},{8,16},{16,8},{24,0},{1,25},{9,17},{17,9},{25,1},{2,26},{10... | collective-permute-start | bytes 3932168 | tf_op jit(solution)/shard_map/ppermute | solution.py:28
  144.9 53.2 %all-to-all-start.5 = ((bf16[4,32,2560]{2,1,0:T(8,128)(2,1)}), bf16[4,32,2560]{2,1,0:T(8,128)(2,1)S(1)}, u32[]{:S(2)}, u32[]{:S(2)}) async-start(bf16[4,32,2560]{2,1,0:T(8,128)(2,1)} %bitcast.95), calls=%async_computation.5 | async-start | bytes 1310720 | tf_op jit(solution)/shard_map/all_to_all | solution.py:32
  193.7 14.5 %collective-permute-start.18 = (f32[16,16]{1,0:T(8,128)S(1)}, f32[16,16]{1,0:T(8,128)S(1)}, u32[]{:S(2)}, u32[]{:S(2)}) collective-permute-start(f32[16,16]{1,0:T(8,128)S(1)} %select_reduce_fusion), channel_id=1, source_target_pairs={{0,3},{1,2},{2,1},{3,0},{4,7},{5,6},{6,5},{7,4},{8,11},{9,10},{10,... | collective-permute-start | bytes 3080 | tf_op jit(solution)/shard_map/ppermute | solution.py:28
  197.1 11.1 %collective-permute-start.17 = (f32[16,16]{1,0:T(8,128)S(1)}, f32[16,16]{1,0:T(8,128)S(1)}, u32[]{:S(2)}, u32[]{:S(2)}) collective-permute-start(f32[16,16]{1,0:T(8,128)S(1)} %select_reduce_fusion), channel_id=1, source_target_pairs={{0,2},{1,3},{2,0},{3,1},{4,6},{5,7},{6,4},{7,5},{8,10},{9,11},{10,... | collective-permute-start | bytes 3080 | tf_op jit(solution)/shard_map/ppermute | solution.py:28
  197.1 11.1 %collective-permute-start.16 = (f32[16,16]{1,0:T(8,128)S(1)}, f32[16,16]{1,0:T(8,128)S(1)}, u32[]{:S(2)}, u32[]{:S(2)}) collective-permute-start(f32[16,16]{1,0:T(8,128)S(1)} %select_reduce_fusion), channel_id=1, source_target_pairs={{0,1},{1,0},{2,3},{3,2},{4,5},{5,4},{6,7},{7,6},{8,9},{9,8},{10,11... | collective-permute-start | bytes 3080 | tf_op jit(solution)/shard_map/ppermute | solution.py:28
  208.2 18.4 %collective-permute-start.19 = (f32[4,2,16]{2,1,0:T(2,128)S(1)}, f32[4,2,16]{2,1,0:T(2,128)S(1)}, u32[]{:S(2)}, u32[]{:S(2)}) collective-permute-start(f32[4,2,16]{2,1,0:T(2,128)S(1)} %get-tuple-element.21), channel_id=1, source_target_pairs={{0,4},{4,0},{1,5},{5,1},{2,6},{6,2},{3,7},{7,3},{8,12},{12,8},{9,1... | collective-permute-start | bytes 1544 | tf_op jit(solution)/shard_map/ppermute | solution.py:28
  222.0 14.9 %all-to-all-start.7 = ((bf16[4,128,512]{2,1,0:T(8,128)(2,1)}), bf16[4,128,512]{2,1,0:T(8,128)(2,1)S(1)}, u32[]{:S(2)}, u32[]{:S(2)}) async-start(bf16[4,128,512]{2,1,0:T(8,128)(2,1)} %output_terms.3), calls=%async_computation.7 | async-start | bytes 1048576 | tf_op jit(solution)/shard_map/all_to_all | solution.py:32
  (21 other events, 182.5 us)
